TPU v7x, 32 devices: a whole 2x2x4 slice. The times are simulated.
32 devices in a mesh: rep: 2 (over x), seq: 16 (over z, y, core).
Axes of the slice: x: 2, y: 2, z: 4, core: 2. Of those that a mesh axis runs over, the one named last changes fastest.
Arguments:
- queries: bfloat16 [32, 32, 5120], P('seq', 'rep'), parts along dimension 1, may hold values from -4 to 4
- key_states: bfloat16 [32, 32, 5120], P('seq', 'rep'), parts along dimension 1, may hold values from -6 to 6
- value_states: bfloat16 [32, 32, 5120], P('seq', 'rep'), parts along dimension 1, may hold values from -6 to 6
- hidden: bfloat16 [32, 32, 5120], P('seq', 'rep'), parts along dimension 1, may hold values from -6 to 6
- residual_gate: float32 [32, 5120], P('rep'), parts along dimension 0, may hold values from 0.5 to 1.5
- head_shift: float32 [32, 5120], P('rep'), parts along dimension 0, may hold values from -3 to 3
- head_scale: float32 [32, 5120], P('rep'), parts along dimension 0, may hold values from -1.5 to 1.5
- head_weight: bfloat16 [5120, 64], replicated, may hold values from -0.078125 to 0.078125
- head_bias: float32 [64], replicated, may hold values from -3 to 3
- guidance: float32 [16], P('rep'), parts along dimension 0, may hold values from 3 to 7
- step_index: int32 [16], P('rep'), parts along dimension 0, may hold values from 0 to 9
- lengths: int32 [16], P('rep'), parts along dimension 0, may hold values from 1 to 32, 128 in all
- latent: float32 [32, 16, 64], P('seq', 'rep'), parts along dimension 1, may hold values from -6 to 6
- embed_weight: bfloat16 [64, 5120], replicated, may hold values from -0.75 to 0.75
- embed_bias: float32 [5120], replicated, may hold values from -3 to 3
- adapter_ids: int32 [16], P('rep'), parts along dimension 0, may hold values from 0 to 15
- adapter_down: bfloat16 [16, 5120, 64], P('seq'), may hold values from -0.078125 to 0.078125
- adapter_up: bfloat16 [16, 15360, 64], P('seq'), may hold values from -0.75 to 0.75
Outputs:
- velocity: float32 [32, 16, 64], P('seq', 'rep'), parts along dimension 1
- latent_next: float32 [32, 16, 64], P('seq', 'rep'), parts along dimension 1
- adapter_delta: bfloat16 [32, 16, 15360], P(None, 'rep', 'seq'), parts along dimension 1
There are 2 independent parts, one for each index of `rep`. A program takes and returns all parts, laid end to end along the dimension named above; an argument that names none is the same for every part. Nothing has to cross between parts.
All inputs are finite; a program needn't handle non-finite values.
Results may differ from a plain program's by a relative error of at most 0.0066.
Values may be sent and summed in bfloat16 or wider, within the bound.
No kernel may reach another device: no remote copies, remote signals or barrier semaphores. Data moves between devices by JAX's collectives and lax.ppermute only.
A program may use at most 128 MiB of HBM per device.

v0:
```python
import jax
import jax.numpy as jnp
from jax import lax
from jax.sharding import PartitionSpec as P

HEADS = 40
HEAD_DIM = 128
REQUESTS = 8
STEPS = 10


def broadcast(value, axis, source):
    kept = jnp.where(lax.axis_index(axis) == source, value, 0).astype(value.dtype)
    return lax.psum(kept, axis)


def noise_level(position):
    fraction = 1.0 - position / STEPS
    return 5.0 * fraction / (1.0 + 4.0 * fraction)


def layer_normed(rows):
    row_mean = jnp.mean(rows, axis=-1, keepdims=True)
    centered = rows - row_mean
    row_var = jnp.mean(centered * centered, axis=-1, keepdims=True)
    return centered * lax.rsqrt(row_var + 1e-06)


def shards(
    queries,
    key_states,
    value_states,
    hidden,
    residual_gate,
    head_shift,
    head_scale,
    head_weight,
    head_bias,
    guidance,
    step_index,
    lengths,
    latent,
    embed_weight,
    embed_bias,
    adapter_ids,
    adapter_down,
    adapter_up,
):
    row_count, stream_count, feature_width = queries.shape
    axis_devices = lax.axis_size("seq")
    full_length = row_count * axis_devices
    item_count = stream_count * feature_width // HEAD_DIM
    local_items = item_count // axis_devices
    score_scale = 1.0 / HEAD_DIM**0.5

    def as_items(states):
        return states.reshape(row_count, item_count, HEAD_DIM)

    query_heads, key_heads, value_heads = (
        lax.all_to_all(as_items(queries), "seq", split_axis=1, concat_axis=0, tiled=True),
        lax.all_to_all(as_items(key_states), "seq", split_axis=1, concat_axis=0, tiled=True),
        lax.all_to_all(as_items(value_states), "seq", split_axis=1, concat_axis=0, tiled=True),
    )
    first_item = lax.axis_index("seq") * local_items
    item_request = (first_item + jnp.arange(local_items)) // HEADS % REQUESTS
    selector = (item_request[:, None] == jnp.arange(REQUESTS)[None, :]).astype(jnp.int32)
    key_limit = jnp.sum(selector * lengths[None, :], axis=1)

    def attend(operands):
        query_rows, key_rows, value_rows, key_bound = operands
        scores = (
            jnp.einsum("qd,kd->qk", query_rows, key_rows, preferred_element_type=jnp.float32)
            * score_scale
        )
        allowed = jnp.arange(full_length)[None, :] < key_bound
        scores = jnp.where(allowed, scores, -jnp.inf)
        weights = jax.nn.softmax(scores, axis=-1).astype(jnp.bfloat16)
        return jnp.dot(weights, value_rows, preferred_element_type=jnp.float32).astype(jnp.bfloat16)

    attended_items = lax.map(
        attend,
        (
            jnp.moveaxis(query_heads, 1, 0),
            jnp.moveaxis(key_heads, 1, 0),
            jnp.moveaxis(value_heads, 1, 0),
            key_limit,
        ),
    )
    returned = lax.all_to_all(
        jnp.moveaxis(attended_items, 0, 1), "seq", split_axis=0, concat_axis=1, tiled=True
    )
    attended = returned.reshape(row_count, stream_count, feature_width)
    residual = hidden.astype(jnp.float32) + residual_gate[None, :, :] * attended.astype(jnp.float32)
    normed = (layer_normed(residual) * (1.0 + head_scale[None]) + head_shift[None]).astype(
        jnp.bfloat16
    )
    stream_velocity = jnp.dot(
        normed.reshape(-1, feature_width), head_weight, preferred_element_type=jnp.float32
    )
    stream_velocity = stream_velocity.reshape(row_count, stream_count, -1) + head_bias
    conditional = stream_velocity[:, :REQUESTS]
    unconditional = stream_velocity[:, REQUESTS:]
    velocity = unconditional + guidance[None, :, None] * (conditional - unconditional)
    sigma_now = noise_level(step_index.astype(jnp.float32))
    sigma_next = noise_level((step_index + 1).astype(jnp.float32))
    latent_next = latent + (sigma_next - sigma_now)[None, :, None] * velocity
    latent_rounded = latent_next.astype(jnp.bfloat16)
    held_slots = adapter_down.shape[0]
    embedded = jnp.dot(
        latent_rounded.reshape(row_count * REQUESTS, -1),
        embed_weight,
        preferred_element_type=jnp.float32,
    )
    embedded = embedded.reshape(row_count, REQUESTS, feature_width) + embed_bias
    block_input = layer_normed(embedded).astype(jnp.bfloat16)
    up_parts = lax.all_to_all(adapter_up, "seq", split_axis=1, concat_axis=0, tiled=True)
    user_count = up_parts.shape[0]
    chooser = (adapter_ids[:, None] == jnp.arange(user_count)[None, :]).astype(jnp.bfloat16)
    up_used = jnp.einsum(
        "ru,uck->rck", chooser, up_parts, preferred_element_type=jnp.float32
    ).astype(jnp.bfloat16)
    down_list = []
    for request in range(REQUESTS):
        owner_device = adapter_ids[request] // held_slots
        owner_slot = adapter_ids[request] % held_slots
        own_down = lax.dynamic_index_in_dim(adapter_down, owner_slot, 0, keepdims=False)
        whole_down = broadcast(own_down, "seq", owner_device)
        down_list.append(whole_down)
    down_used = jnp.stack(down_list, axis=0)
    low_rank = jnp.einsum(
        "lrd,rdk->lrk", block_input, down_used, preferred_element_type=jnp.float32
    ).astype(jnp.bfloat16)
    low_rank_all = lax.all_gather(low_rank, "seq", axis=0, tiled=True)
    adapter_delta = jnp.einsum(
        "lrk,rck->lrc", low_rank_all, up_used, preferred_element_type=jnp.float32
    ).astype(jnp.bfloat16)
    return (velocity, latent_next, adapter_delta)


def solution(mesh):
    placed = (
        P("seq", "rep", None),
        P("seq", "rep", None),
        P("seq", "rep", None),
        P("seq", "rep", None),
        P("rep", None),
        P("rep", None),
        P("rep", None),
        P(),
        P(),
        P("rep"),
        P("rep"),
        P("rep"),
        P("seq", "rep", None),
        P(),
        P(),
        P("rep"),
        P("seq", None, None),
        P("seq", None, None),
    )
    return jax.shard_map(
        shards,
        mesh=mesh,
        in_specs=placed,
        out_specs=(P("seq", "rep", None), P("seq", "rep", None), P(None, "rep", "seq")),
        check_vma=False,
    )
```

profile of v0, /device:TPU:9, one launch (start us, length us, event | category | flops | bytes accessed | tf_op | source)
XLA Modules:
  0.0 412.2 jit_solution(12641059591133718054)
XLA Ops:
  9.5 6.6 %all-to-all-start = ((bf16[2,640,128]{2,0,1:T(2,128)(2,1)}), bf16[2,640,128]{2,0,1:T(2,128)(2,1)S(1)}, u32[]{:S(2)}, u32[]{:S(2)}) async-start(bf16[2,640,128]{2,0,1:T(2,128)(2,1)} %copy.74), calls=%async_computation | async-start | bytes 655360 | tf_op jit(solution)/shard_map/all_to_all | solution.py:60
  18.3 7.8 %all-to-all-done = bf16[2,640,128]{2,0,1:T(2,128)(2,1)S(1)} async-done(((bf16[2,640,128]{2,0,1:T(2,128)(2,1)}), bf16[2,640,128]{2,0,1:T(2,128)(2,1)S(1)}, u32[]{:S(2)}, u32[]{:S(2)}) %all-to-all-start) | async-done | bytes 327712 | tf_op jit(solution)/shard_map/all_to_all | solution.py:60
  26.1 4.5 %all-to-all-start.1 = ((bf16[2,640,128]{2,0,1:T(2,128)(2,1)}), bf16[2,640,128]{2,0,1:T(2,128)(2,1)S(1)}, u32[]{:S(2)}, u32[]{:S(2)}) async-start(bf16[2,640,128]{2,0,1:T(2,128)(2,1)} %copy.77), calls=%async_computation.1 | async-start | bytes 655360 | tf_op jit(solution)/shard_map/all_to_all | solution.py:61
  30.6 1.6 fusion.37
  40.7 5.1 %all-to-all-start.2 = ((bf16[2,640,128]{2,0,1:T(2,128)(2,1)}), bf16[2,640,128]{2,0,1:T(2,128)(2,1)}, u32[]{:S(2)}, u32[]{:S(2)}) async-start(bf16[2,640,128]{2,0,1:T(2,128)(2,1)} %copy.80), calls=%async_computation.2 | async-start | bytes 655360 | tf_op jit(solution)/shard_map/all_to_all | solution.py:62
  45.9 2.4 broadcast_select_fusion
  49.5 6.6 %all-to-all-done.2 = bf16[2,640,128]{2,0,1:T(2,128)(2,1)} async-done(((bf16[2,640,128]{2,0,1:T(2,128)(2,1)}), bf16[2,640,128]{2,0,1:T(2,128)(2,1)}, u32[]{:S(2)}, u32[]{:S(2)}) %all-to-all-start.2) | async-done | bytes 327712 | tf_op jit(solution)/shard_map/all_to_all | solution.py:62
  57.9 144.0 %while.10 = (s32[]{:T(128)}, bf16[40,32,128]{2,1,0:T(8,128)(2,1)}, s32[40]{0:T(128)S(1)}, bf16[40,32,128]{2,1,0:T(8,128)(2,1)}, bf16[40,32,128]{2,1,0:T(8,128)(2...) while((s32[]{:T(128)}, bf16[40,32,128]{2,1,0:T(8,128)(2,1)}, s32[40]{0:T(128)S(1)}, ...), condition=%wide.region_4.5_spmd, body=%wide.region_1.4_spmd.sunk | while | flops 536546 | bytes 48381 | solution.py:80
  60.0 1.5 fusion.48
  63.6 1.5 fusion.48
  67.2 1.5 fusion.48
  70.8 1.5 fusion.48
  74.4 1.5 fusion.48
  78.0 1.5 fusion.48
  81.6 1.5 fusion.48
  85.2 1.5 fusion.48
  88.8 1.5 fusion.48
  92.4 1.5 fusion.48
  96.0 1.5 fusion.48
  99.6 1.5 fusion.48
  103.2 1.5 fusion.48
  110.4 1.5 fusion.48
  114.0 1.5 fusion.48
  121.2 1.5 fusion.48
  124.8 1.5 fusion.48
  128.4 1.5 fusion.48
  135.6 1.5 fusion.48
  139.2 1.5 fusion.48
  142.8 1.5 fusion.48
  146.4 1.5 fusion.48
  150.0 1.5 fusion.48
  153.6 1.5 fusion.48
  157.2 1.5 fusion.48
  160.8 1.5 fusion.48
  164.4 1.5 fusion.48
  168.0 1.5 fusion.48
  171.6 1.5 fusion.48
  201.8 1.8 copy.113
  203.7 4.5 %all-to-all-start.3 = ((bf16[32,40,128]{2,1,0:T(8,128)(2,1)}), bf16[32,40,128]{2,1,0:T(8,128)(2,1)S(1)}, u32[]{:S(2)}, u32[]{:S(2)}) async-start(bf16[32,40,128]{2,1,0:T(8,128)(2,1)} %bitcast.75), calls=%async_computation.3 | async-start | bytes 655360 | tf_op jit(solution)/shard_map/all_to_all | solution.py:89
  209.0 11.8 %copy.88 = bf16[1,15360,64]{2,0,1:T(2,128)(2,1)} copy(bf16[1,15360,64]{1,2,0:T(8,128)(2,1)S(1)} %copy-done.1) | data formatting | bytes 3932160 | tf_op args[17]
  221.2 85.3 %reduce = bf16[15360,64]{1,0:T(8,128)(2,1)} reduce(bf16[15360,1,64]{2,1,0:T(2,128)(2,1)} %bitcast.87, bf16[]{:T(256)} %broadcast.198), dimensions={1}, to_apply=%bitcast.65.reduce_sub_computation | reduce | bytes 3932162
  306.6 7.2 %reshape.137 = bf16[16,2,30720]{2,1,0:T(2,128)(2,1)} reshape(bf16[15360,64]{1,0:T(8,128)(2,1)} %reduce) | data formatting | bytes 3932160
  313.8 6.1 %all-to-all-start.4 = ((bf16[16,2,30720]{2,1,0:T(2,128)(2,1)}), bf16[16,2,30720]{2,1,0:T(2,128)(2,1)S(1)}, u32[]{:S(2)}, u32[]{:S(2)}) async-start(bf16[16,2,30720]{2,1,0:T(2,128)(2,1)} %reshape.137), calls=%async_computation.4 | async-start | bytes 3932160 | tf_op jit(solution)/shard_map/all_to_all | solution.py:116
  325.0 2.0 convolution_add_fusion.1
  334.7 40.3 %all_gather.3 = bf16[32,8,64]{2,1,0:T(8,128)(2,1)S(1)} all-gather(bf16[2,8,64]{2,1,0:T(8,128)(2,1)S(1)} %copy.91), channel_id=1, replica_groups=mesh['rep'=2,'seq'=16] {'seq'}, dimensions={0}, use_global_device_ids=true | all-gather | bytes 34816 | tf_op jit(solution)/shard_map/all_gather | solution.py:133
  375.0 8.2 %reshape.138 = bf16[15360,1,64]{2,1,0:T(2,128)(2,1)} reshape(bf16[16,2,30720]{2,1,0:T(2,128)(2,1)S(1)} %all-to-all-done.4) | data formatting | bytes 3932160
  383.2 15.5 %copy.89 = bf16[1,15360,64]{1,2,0:T(8,128)(2,1)} copy(bf16[1,15360,64]{2,0,1:T(2,128)(2,1)} %bitcast.86) | data formatting | bytes 3932160 | tf_op jit(solution)/shard_map/all_to_all | solution.py:116
  398.7 3.8 all_to_all.69
  (255 shorter events, 128.3 us)
Async XLA Ops:
  7.2 320.5 %copy-start = (bf16[64,5120]{1,0:T(8,128)(2,1)S(1)}, bf16[64,5120]{1,0:T(8,128)(2,1)}, u32[]{:S(2)}) copy-start(bf16[64,5120]{1,0:T(8,128)(2,1)} %param.33) | copy-start | bytes 1966084
  7.2 38.7 %copy-start.2 = (bf16[1,5120,64]{1,2,0:T(8,128)(2,1)S(1)}, bf16[1,5120,64]{1,2,0:T(8,128)(2,1)}, u32[]{:S(2)}) copy-start(bf16[1,5120,64]{1,2,0:T(8,128)(2,1)} %param.36) | copy-start | bytes 1966084
  9.5 16.6 %all-to-all-start = ((bf16[2,640,128]{2,0,1:T(2,128)(2,1)}), bf16[2,640,128]{2,0,1:T(2,128)(2,1)S(1)}, u32[]{:S(2)}, u32[]{:S(2)}) async-start(bf16[2,640,128]{2,0,1:T(2,128)(2,1)} %copy.74), calls=%async_computation | async-start | bytes 655360 | tf_op jit(solution)/shard_map/all_to_all | solution.py:60
  26.1 14.6 %all-to-all-start.1 = ((bf16[2,640,128]{2,0,1:T(2,128)(2,1)}), bf16[2,640,128]{2,0,1:T(2,128)(2,1)S(1)}, u32[]{:S(2)}, u32[]{:S(2)}) async-start(bf16[2,640,128]{2,0,1:T(2,128)(2,1)} %copy.77), calls=%async_computation.1 | async-start | bytes 655360 | tf_op jit(solution)/shard_map/all_to_all | solution.py:61
  40.7 15.3 %all-to-all-start.2 = ((bf16[2,640,128]{2,0,1:T(2,128)(2,1)}), bf16[2,640,128]{2,0,1:T(2,128)(2,1)}, u32[]{:S(2)}, u32[]{:S(2)}) async-start(bf16[2,640,128]{2,0,1:T(2,128)(2,1)} %copy.80), calls=%async_computation.2 | async-start | bytes 655360 | tf_op jit(solution)/shard_map/all_to_all | solution.py:62
  45.9 2.5 copy-start.14
  45.9 282.4 %all-reduce.3.cloned.1.call-start = ((), (), s32[]{:S(2)}) async-start(), calls=%async_computation.5 | async-start | bytes 10485760 | tf_op jit(solution)/shard_map/psum | solution.py:14
  48.3 160.7 %copy-start.1 = (bf16[1,15360,64]{1,2,0:T(8,128)(2,1)S(1)}, bf16[1,15360,64]{1,2,0:T(8,128)(2,1)}, u32[]{:S(2)}) copy-start(bf16[1,15360,64]{1,2,0:T(8,128)(2,1)} %param.37) | copy-start | bytes 5898244
  49.4 158.8 %copy-start.7 = (f32[16,5120]{1,0:T(8,128)S(1)}, f32[16,5120]{1,0:T(8,128)}, u32[]{:S(2)}) copy-start(f32[16,5120]{1,0:T(8,128)} %param.26) | copy-start | bytes 983044
  203.7 110.1 %all-to-all-start.3 = ((bf16[32,40,128]{2,1,0:T(8,128)(2,1)}), bf16[32,40,128]{2,1,0:T(8,128)(2,1)S(1)}, u32[]{:S(2)}, u32[]{:S(2)}) async-start(bf16[32,40,128]{2,1,0:T(8,128)(2,1)} %bitcast.75), calls=%async_computation.3 | async-start | bytes 655360 | tf_op jit(solution)/shard_map/all_to_all | solution.py:89
  306.6 7.2 %copy-start.15 = (s32[8]{0:T(128)S(1)}, s32[8]{0:T(128)}, u32[]{:S(2)}) copy-start(s32[8]{0:T(128)} %param.30) | copy-start | bytes 100
  313.7 11.2 %copy-start.12 = (f32[64]{0:T(128)S(1)}, f32[64]{0:T(128)}, u32[]{:S(2)}) copy-start(f32[64]{0:T(128)} %param.28) | copy-start | bytes 772
  313.7 13.2 %copy-start.11 = (f32[2,8,64]{2,1,0:T(8,128)S(1)}, f32[2,8,64]{2,1,0:T(8,128)}, u32[]{:S(2)}) copy-start(f32[2,8,64]{2,1,0:T(8,128)} %param.32) | copy-start | bytes 12292
  313.7 13.2 %copy-start.13 = (f32[8]{0:T(128)S(1)}, f32[8]{0:T(128)}, u32[]{:S(2)}) copy-start(f32[8]{0:T(128)} %param.29) | copy-start | bytes 100
  313.8 13.9 %copy-start.10 = (f32[5120]{0:T(1024)S(1)}, f32[5120]{0:T(1024)}, u32[]{:S(2)}) copy-start(f32[5120]{0:T(1024)} %param.34) | copy-start | bytes 61444
  313.8 61.3 %all-to-all-start.4 = ((bf16[16,2,30720]{2,1,0:T(2,128)(2,1)}), bf16[16,2,30720]{2,1,0:T(2,128)(2,1)S(1)}, u32[]{:S(2)}, u32[]{:S(2)}) async-start(bf16[16,2,30720]{2,1,0:T(2,128)(2,1)} %reshape.137), calls=%async_computation.4 | async-start | bytes 3932160 | tf_op jit(solution)/shard_map/all_to_all | solution.py:116
  327.6 5.6 %copy-start.9 = (f32[2,8,64]{2,1,0:T(8,128)}, f32[2,8,64]{2,1,0:T(8,128)S(1)}, u32[]{:S(2)}) copy-start(f32[2,8,64]{2,1,0:T(8,128)S(1)} %get-tuple-element.98) | copy-start | bytes 12292
  328.3 4.7 %copy-start.6 = (bf16[1,5120,64]{1,2,0:T(8,128)(2,1)S(1)}, bf16[1,5120,64]{1,2,0:T(8,128)(2,1)}, u32[]{:S(2)}) copy-start(bf16[1,5120,64]{1,2,0:T(8,128)(2,1)} %get-tuple-element.94) | copy-start | bytes 1966084
  328.3 4.8 %copy-start.5 = (bf16[1,5120,64]{1,2,0:T(8,128)(2,1)S(1)}, bf16[1,5120,64]{1,2,0:T(8,128)(2,1)}, u32[]{:S(2)}) copy-start(bf16[1,5120,64]{1,2,0:T(8,128)(2,1)} %get-tuple-element.95) | copy-start | bytes 1966084
  328.3 4.8 %copy-start.4 = (bf16[1,5120,64]{1,2,0:T(8,128)(2,1)S(1)}, bf16[1,5120,64]{1,2,0:T(8,128)(2,1)}, u32[]{:S(2)}) copy-start(bf16[1,5120,64]{1,2,0:T(8,128)(2,1)} %get-tuple-element.96) | copy-start | bytes 1966084
  328.3 4.9 %copy-start.3 = (bf16[1,5120,64]{1,2,0:T(8,128)(2,1)S(1)}, bf16[1,5120,64]{1,2,0:T(8,128)(2,1)}, u32[]{:S(2)}) copy-start(bf16[1,5120,64]{1,2,0:T(8,128)(2,1)} %get-tuple-element.97) | copy-start | bytes 1966084
  383.2 19.3 %copy-start.8 = (s32[8]{0:T(128)S(1)}, s32[8]{0:T(128)}, u32[]{:S(2)}) copy-start(s32[8]{0:T(128)} %param.35) | copy-start | bytes 100
Sparse Core Ops, SparseCore 0:
  51.4 127.9 all-reduce.2
where the time goes:
time: 418 us; the launch traced here: 412 us
  other arithmetic  120 us (29%)
  matrix products  98.7 us (24%)
  local copies, waits for them, and re-layouts  90.6 us (22%)
  blocking collectives  40.3 us (10%)
  starting transfers between devices  26.9 us (6%)
  between operations  19.4 us (5%)
  waiting for transfers between devices  15.7 us (4%)
    unnamed x1, other arithmetic  85.3 us
    dot_general x40, matrix products, attend(): jnp.dot(weights, value_rows, preferred_element_type=jnp.float32)  59.4 us
    all_gather x1, blocking collectives, shards(): low_rank_all = lax.all_gather(low_rank, 'seq', axis=0, tiled=True)  40.3 us
    dot_general x40, matrix products, attend(): jnp.einsum('qd,kd->qk', query_rows, key_rows, preferred_element_type=jnp....  33.7 us
    unnamed x44, local copies, waits for them, and re-layouts  33.6 us
    lt x40, other arithmetic, attend(): allowed = jnp.arange(full_length)[None, :] < key_bound  26 us
    dynamic_slice x40, local copies, waits for them, and re-layouts, shards(): lax.map(attend, (jnp.moveaxis(query_heads, 1, 0), jnp.moveaxis(key_heads,...  23.3 us
    all_to_all x2, local copies, waits for them, and re-layouts, shards(): lax.all_to_all(adapter_up, 'seq', split_axis=1, concat_axis=0, tiled=True)  19.3 us
  transfers between devices with their start and end apart: 6, of which 3 were waited for; matrix products, arithmetic and copies ran while one was open for 67% of the time, Pallas kernels for 0%

commit v1 on v0

--- a/solution.py
+++ b/solution.py
@@ -1,12 +1,321 @@
+import functools
+
 import jax
 import jax.numpy as jnp
 from jax import lax
+from jax.experimental import pallas as pl
+from jax.experimental.pallas import tpu as pltpu
 from jax.sharding import PartitionSpec as P
 
 HEADS = 40
 HEAD_DIM = 128
 REQUESTS = 8
 STEPS = 10
+LANES = 128
+QUARTERS = 4
+TABLE_ROWS = 72
+VMEM_LIMIT = 56 << 20
+
+NT = (((1,), (1,)), ((), ()))
+
+
+def nt_dot(a, b):
+    return lax.dot_general(a, b, NT, preferred_element_type=jnp.float32)
+
+
+def prepare_kernel(
+    place_ref,
+    q_ref,
+    k_ref,
+    v_ref,
+    h_ref,
+    embed_ref,
+    bias_ref,
+    down_ref,
+    up_ref,
+    send_ref,
+    gram_ref,
+    *,
+    devices,
+    columns,
+    half_tiles,
+):
+    row_count, stream_count, width = q_ref.shape
+    quarter = width // QUARTERS
+    tiles = quarter // LANES
+    table_rows = half_tiles * TABLE_ROWS
+    size = stream_count * 8
+    to = lax.broadcasted_iota(jnp.int32, (size, size), 0)
+    at = lax.broadcasted_iota(jnp.int32, (size, size), 1)
+    same = (to // 8 == at % stream_count) & (to % 8 == at // stream_count)
+    permutation = jnp.where(same, 1.0, 0.0).astype(jnp.bfloat16)
+    for kind, ref in enumerate((q_ref, k_ref, v_ref, h_ref)):
+        stacked = jnp.concatenate(
+            [
+                ref[token, :, part * quarter : (part + 1) * quarter]
+                for part in range(QUARTERS)
+                for token in range(row_count)
+            ],
+            axis=0,
+        )
+        moved = jnp.dot(permutation, stacked, preferred_element_type=jnp.float32)
+        moved = moved.astype(jnp.bfloat16)
+        for tile in range(tiles):
+            first = table_rows + (kind * tiles + tile) * 8
+            send_ref[:, first : first + 8, :] = moved[
+                :, tile * LANES : (tile + 1) * LANES
+            ].reshape(stream_count, 8, LANES)
+
+    bias = bias_ref[...]
+    high = bias.astype(jnp.bfloat16).astype(jnp.float32)
+    middle = (bias - high).astype(jnp.bfloat16).astype(jnp.float32)
+    low = bias - high - middle
+    row = lax.broadcasted_iota(jnp.int32, (16, width), 0)
+    extra = jnp.where(row == 0, high, jnp.where(row == 1, middle, jnp.where(row == 2, low, 0.0)))
+    extra = jnp.where(row == 3, 1.0, extra).astype(jnp.bfloat16)
+    rows = jnp.concatenate([embed_ref[...], extra], axis=0)
+    raw = nt_dot(rows, down_ref[...])
+    gram = nt_dot(rows, rows)
+    ones_at = 67
+    sums = gram[:, ones_at : ones_at + 1]
+    centered = raw - sums * (1.0 / width) * raw[ones_at : ones_at + 1, :]
+    gram_ref[...] = gram - sums * (1.0 / width) * gram[ones_at : ones_at + 1, :]
+    bias_row = centered[64:65] + centered[65:66] + centered[66:67]
+    tail = lax.broadcasted_iota(jnp.int32, (8, centered.shape[1]), 0)
+    mixing = jnp.concatenate(
+        [centered[:64], jnp.where(tail == 0, jnp.broadcast_to(bias_row, tail.shape), 0.0)], axis=0
+    )
+    mixing_high = mixing.astype(jnp.bfloat16)
+    mixing_low = (mixing - mixing_high.astype(jnp.float32)).astype(jnp.bfloat16)
+    mixing = jnp.concatenate([mixing_high, mixing_low], axis=1)
+
+    half = half_tiles * LANES
+    side = place_ref[1] * half
+    for target in range(devices):
+        start = columns * target // LANES * LANES
+        part = up_ref[:, pl.ds(pl.multiple_of(start + side, LANES), half)]
+        table = jnp.dot(
+            mixing, jnp.concatenate([part, part], axis=0), preferred_element_type=jnp.float32
+        ).astype(jnp.bfloat16)
+        for tile in range(half_tiles):
+            send_ref[target, tile * TABLE_ROWS : (tile + 1) * TABLE_ROWS, :] = table[
+                :, tile * LANES : (tile + 1) * LANES
+            ]
+
+
+def select_kernel(ids_ref, table_ref, out_ref):
+    out_ref[...] = table_ref[...]
+
+
+def group_sum(x):
+    grouped = x.reshape(x.shape[0] // 8, 8, x.shape[1])
+    grouped = grouped + pltpu.roll(grouped, 2, 1)
+    grouped = grouped + pltpu.roll(grouped, 4, 1)
+    return grouped.reshape(x.shape)
+
+
+def attend_kernel(
+    place_ref,
+    lengths_ref,
+    got_ref,
+    gate_ref,
+    shift_ref,
+    scale_ref,
+    weight_ref,
+    bias_ref,
+    latent_ref,
+    out_ref,
+    residual_ref,
+    pick_ref,
+    *,
+    table_rows,
+):
+    devices = got_ref.shape[0]
+    width = gate_ref.shape[1]
+    quarter = width // QUARTERS
+    tiles = quarter // LANES
+    size = devices * 8
+    mine = place_ref[0]
+    limit = lengths_ref[mine % REQUESTS]
+    score_scale = 1.0 / HEAD_DIM**0.5
+
+    row = lax.broadcasted_iota(jnp.int32, (size, size), 0)
+    column = lax.broadcasted_iota(jnp.int32, (size, size), 1)
+    key_token = column // 8 * 2 + column % 2
+    allowed = (row % 8 // 2 == column % 8 // 2) & (key_token < limit)
+    part_of_row = lax.broadcasted_iota(jnp.int32, (8, LANES), 0) // 2
+
+    def own_row(ref):
+        block = ref[pl.ds(pl.multiple_of(mine // 8 * 8, 8), 8), :]
+        return pltpu.roll(block, (8 - mine % 8) % 8, 0)[0:1]
+
+    gate, shift, scale = own_row(gate_ref), own_row(shift_ref), own_row(scale_ref)
+
+    def per_row(values, tile):
+        value = jnp.zeros((8, LANES), jnp.float32)
+        for part in range(QUARTERS):
+            first = part * quarter + tile * LANES
+            piece = values[:, first : first + LANES]
+            value = jnp.where(part_of_row == part, jnp.broadcast_to(piece, (8, LANES)), value)
+        return value
+
+    def widened(value):
+        return jnp.broadcast_to(value[None], (devices, 8, LANES)).reshape(size, LANES)
+
+    total = jnp.zeros((size, LANES), jnp.float32)
+    for tile in range(tiles):
+        q, k, v, h = [
+            got_ref[
+                :,
+                table_rows + (kind * tiles + tile) * 8 : table_rows + (kind * tiles + tile) * 8 + 8,
+                :,
+            ].reshape(size, LANES)
+            for kind in range(4)
+        ]
+        scores = jnp.where(allowed, nt_dot(q, k) * score_scale, -jnp.inf)
+        peak = jnp.max(scores, axis=-1, keepdims=True)
+        raised = jnp.exp(scores - peak)
+        weights = raised / jnp.sum(raised, axis=-1, keepdims=True)
+        attended = jnp.dot(
+            weights.astype(jnp.bfloat16), v, preferred_element_type=jnp.float32
+        ).astype(jnp.bfloat16)
+        residual = h.astype(jnp.float32) + widened(per_row(gate, tile)) * attended.astype(
+            jnp.float32
+        )
+        residual_ref[tile] = residual
+        total = total + residual
+    mean = jnp.sum(group_sum(total), axis=-1, keepdims=True) * (1.0 / width)
+    total = jnp.zeros((size, LANES), jnp.float32)
+    for tile in range(tiles):
+        centered = residual_ref[tile] - mean
+        residual_ref[tile] = centered
+        total = total + centered * centered
+    variance = jnp.sum(group_sum(total), axis=-1, keepdims=True) * (1.0 / width)
+    inverse = lax.rsqrt(variance + 1e-06)
+    channels = weight_ref.shape[0]
+    product = jnp.zeros((size, QUARTERS * channels), jnp.float32)
+    for tile in range(tiles):
+        normed = residual_ref[tile] * inverse * widened(
+            1.0 + per_row(scale, tile)
+        ) + widened(per_row(shift, tile))
+        weight = jnp.concatenate(
+            [
+                weight_ref[:, part * quarter + tile * LANES : part * quarter + (tile + 1) * LANES]
+                for part in range(QUARTERS)
+            ],
+            axis=0,
+        )
+        product = product + nt_dot(normed.astype(jnp.bfloat16), weight)
+    row = lax.broadcasted_iota(jnp.int32, product.shape, 0)
+    column = lax.broadcasted_iota(jnp.int32, product.shape, 1)
+    product = jnp.where(row % 8 // 2 == column // channels, product, 0.0)
+    product = group_sum(product[:, :LANES] + product[:, LANES:])
+    product = product + pltpu.roll(product, channels, 1)
+    bias = bias_ref[...]
+    product = product + jnp.concatenate([bias, bias], axis=1)
+    pick_ref[...] = product
+    first_token = pick_ref[pl.ds(0, devices, stride=8), :]
+    second_token = pick_ref[pl.ds(1, devices, stride=8), :]
+    lane = lax.broadcasted_iota(jnp.int32, (devices, LANES), 1)
+    stream_velocity = jnp.where(lane < channels, first_token, second_token)
+    latent = jnp.concatenate([latent_ref[0], latent_ref[1]], axis=1)
+    block = jnp.concatenate([stream_velocity, latent], axis=0)
+    out_ref[...] = jnp.broadcast_to(block[None], out_ref.shape)
+
+
+def finish_kernel(
+    place_ref,
+    ids_ref,
+    got_ref,
+    guidance_ref,
+    step_ref,
+    gram_ref,
+    near_ref,
+    far_ref,
+    velocity_ref,
+    latent_ref,
+    delta_ref,
+    velocity_all,
+    latent_all,
+    product_ref,
+    *,
+    devices,
+    columns,
+    half_tiles,
+):
+    block = devices + REQUESTS
+    guidance = guidance_ref[...]
+    step = step_ref[...]
+    lane = lax.broadcasted_iota(jnp.int32, (REQUESTS, LANES), 1)
+    channels = LANES // 2
+    pieces = []
+    for source in range(devices):
+        conditional = got_ref[pl.ds(source, REQUESTS, stride=block), :]
+        unconditional = got_ref[pl.ds(REQUESTS * block + source, REQUESTS, stride=block), :]
+        velocity = unconditional + guidance * (conditional - unconditional)
+        first = source * block + devices
+        latent_next = got_ref[first : first + REQUESTS, :] + step * velocity
+        velocity_all[source] = velocity
+        latent_all[source] = latent_next
+        tail = jnp.where(lane < channels + 3, 1.0, 0.0)
+        pieces.append(jnp.where(lane < channels, latent_next, tail))
+        pieces.append(jnp.where(lane < channels, pltpu.roll(latent_next, channels, 1), tail))
+    mine = place_ref[0]
+    velocity = velocity_all[mine]
+    latent_next = latent_all[mine]
+    velocity_ref[0] = velocity[:, :channels]
+    velocity_ref[1] = velocity[:, channels:]
+    latent_ref[0] = latent_next[:, :channels]
+    latent_ref[1] = latent_next[:, channels:]
+
+    rounded = jnp.concatenate(pieces, axis=0).astype(jnp.bfloat16)
+    rows = rounded.shape[0]
+    exact = rounded.astype(jnp.float32)
+    used = gram_ref.shape[0]
+    image = jnp.dot(
+        exact[:, :used],
+        gram_ref[...],
+        precision=lax.Precision.HIGHEST,
+        preferred_element_type=jnp.float32,
+    )
+    spread = jnp.sum(image * exact[:, :used], axis=-1, keepdims=True)
+    inverse = lax.rsqrt(spread * (1.0 / (HEADS * HEAD_DIM)) + 1e-06)
+
+    request_of_row = lax.broadcasted_iota(jnp.int32, (rows, TABLE_ROWS), 0) % REQUESTS
+    left = jnp.concatenate(
+        [
+            jnp.where(request_of_row == request, exact[:, :TABLE_ROWS], 0.0)
+            for request in range(REQUESTS)
+        ],
+        axis=1,
+    ).astype(jnp.bfloat16)
+    half = half_tiles * LANES
+    side = place_ref[1]
+    for which, take in (
+        (side, lambda request: near_ref[ids_ref[request]]),
+        (1 - side, lambda request: far_ref[request]),
+    ):
+        tables = [take(request) for request in range(REQUESTS)]
+        right = jnp.concatenate(
+            [
+                jnp.concatenate(
+                    [table[tile * TABLE_ROWS : (tile + 1) * TABLE_ROWS] for table in tables], axis=0
+                )
+                for tile in range(half_tiles)
+            ],
+            axis=1,
+        )
+        product = jnp.dot(left, right, preferred_element_type=jnp.float32) * inverse
+        product_ref[:, pl.ds(pl.multiple_of(which * half, LANES), half)] = product
+    shape = delta_ref.shape
+    offsets = sorted({columns * target % LANES for target in range(devices)})
+    own = columns * mine % LANES
+    for offset in offsets:
+
+        @pl.when(own == offset)
+        def _(offset=offset):
+            kept = product_ref[:, offset : offset + columns]
+            delta_ref[...] = kept.astype(jnp.bfloat16).reshape(shape)
 
 
 def broadcast(value, axis, source):
@@ -26,7 +335,7 @@
     return centered * lax.rsqrt(row_var + 1e-06)
 
 
-def shards(
+def many_per_stream(
     queries,
     key_states,
     value_states,
@@ -137,6 +446,167 @@
     return (velocity, latent_next, adapter_delta)
 
 
+def whole(shape):
+    return pl.BlockSpec(shape, lambda *_: (0,) * len(shape))
+
+
+def one_stream_each(
+    queries,
+    key_states,
+    value_states,
+    hidden,
+    residual_gate,
+    head_shift,
+    head_scale,
+    head_weight,
+    head_bias,
+    guidance,
+    step_index,
+    lengths,
+    latent,
+    embed_weight,
+    embed_bias,
+    adapter_ids,
+    adapter_down,
+    adapter_up,
+):
+    devices = lax.axis_size("seq")
+    row_count, stream_count, width = queries.shape
+    columns = adapter_up.shape[1] // devices
+    half_tiles = window_tiles(columns, devices) // 2
+    table_rows = half_tiles * TABLE_ROWS
+    send_rows = table_rows + 4 * (width // QUARTERS // LANES) * 8
+    place = jnp.stack([lax.axis_index("seq"), lax.axis_index("rep")]).astype(jnp.int32)
+    swap = [(0, 1), (1, 0)]
+    other_ids = lax.ppermute(adapter_ids, "rep", swap)
+    smem = pl.BlockSpec(memory_space=pltpu.SMEM)
+    vmem = pl.BlockSpec(memory_space=pltpu.VMEM)
+    params = pltpu.CompilerParams(vmem_limit_bytes=VMEM_LIMIT)
+
+    send, gram = pl.pallas_call(
+        functools.partial(
+            prepare_kernel, devices=devices, columns=columns, half_tiles=half_tiles
+        ),
+        out_shape=(
+            jax.ShapeDtypeStruct((devices, send_rows, LANES), jnp.bfloat16),
+            jax.ShapeDtypeStruct((80, 80), jnp.float32),
+        ),
+        in_specs=[smem] + [vmem] * 8,
+        out_specs=(vmem, vmem),
+        compiler_params=params,
+        name="prepare",
+    )(
+        place,
+        queries,
+        key_states,
+        value_states,
+        hidden,
+        embed_weight,
+        embed_bias[None, :],
+        adapter_down[0].T,
+        adapter_up[0].T,
+    )
+    got = lax.all_to_all(send, "seq", split_axis=0, concat_axis=0, tiled=True)
+
+    chosen = pl.pallas_call(
+        select_kernel,
+        out_shape=jax.ShapeDtypeStruct((REQUESTS, table_rows, LANES), jnp.bfloat16),
+        grid_spec=pltpu.PrefetchScalarGridSpec(
+            num_scalar_prefetch=1,
+            grid=(REQUESTS,),
+            in_specs=[pl.BlockSpec((1, table_rows, LANES), lambda r, ids: (ids[r], 0, 0))],
+            out_specs=pl.BlockSpec((1, table_rows, LANES), lambda r, ids: (r, 0, 0)),
+        ),
+        name="choose",
+    )(other_ids, got)
+    far = lax.ppermute(chosen, "rep", swap)
+
+    payload_rows = devices + REQUESTS
+    payload = pl.pallas_call(
+        functools.partial(attend_kernel, table_rows=table_rows),
+        out_shape=jax.ShapeDtypeStruct((devices, payload_rows, LANES), jnp.float32),
+        in_specs=[smem, smem] + [vmem] * 7,
+        out_specs=vmem,
+        scratch_shapes=[
+            pltpu.VMEM((width // QUARTERS // LANES, devices * 8, LANES), jnp.float32),
+            pltpu.VMEM((devices * 8, LANES), jnp.float32),
+        ],
+        compiler_params=params,
+        name="attend",
+        cost_estimate=pl.CostEstimate(
+            flops=10**9, bytes_accessed=4 * 10**6, transcendentals=2 * 10**5
+        ),
+    )(
+        place,
+        lengths,
+        got,
+        residual_gate,
+        head_shift,
+        head_scale,
+        head_weight.T,
+        head_bias[None, :],
+        latent,
+    )
+    shared = lax.all_to_all(payload, "seq", split_axis=0, concat_axis=0, tiled=True)
+
+    sigma_now = noise_level(step_index.astype(jnp.float32))
+    sigma_next = noise_level((step_index + 1).astype(jnp.float32))
+    across = (REQUESTS, LANES)
+    return pl.pallas_call(
+        functools.partial(finish_kernel, devices=devices, columns=columns, half_tiles=half_tiles),
+        out_shape=(
+            jax.ShapeDtypeStruct(latent.shape, jnp.float32),
+            jax.ShapeDtypeStruct(latent.shape, jnp.float32),
+            jax.ShapeDtypeStruct((row_count * devices, REQUESTS, columns), jnp.bfloat16),
+        ),
+        in_specs=[smem, smem] + [vmem] * 6,
+        out_specs=(vmem, vmem, vmem),
+        scratch_shapes=[
+            pltpu.VMEM((devices,) + across, jnp.float32),
+            pltpu.VMEM((devices,) + across, jnp.float32),
+            pltpu.VMEM((row_count * devices * REQUESTS, 2 * half_tiles * LANES), jnp.float32),
+        ],
+        compiler_params=params,
+        name="finish",
+    )(
+        place,
+        adapter_ids,
+        shared.reshape(devices * payload_rows, LANES),
+        jnp.broadcast_to(guidance[:, None], across),
+        jnp.broadcast_to((sigma_next - sigma_now)[:, None], across),
+        gram,
+        got,
+        far,
+    )
+
+
+def window_tiles(columns, devices):
+    most = max(
+        pl.cdiv(columns * (d + 1), LANES) - columns * d // LANES for d in range(devices)
+    )
+    return (most + 1) // 2 * 2
+
+
+def shards(*operands):
+    queries, held, table = operands[0], operands[16], operands[17]
+    row_count, stream_count, width = queries.shape
+    devices = lax.axis_size("seq")
+    columns = table.shape[1] // devices
+    fits = (
+        stream_count == devices
+        and row_count == 2
+        and held.shape[0] == 1
+        and held.shape[2] == LANES // 2
+        and lax.axis_size("rep") == 2
+        and width % (QUARTERS * LANES) == 0
+        and all(
+            columns * d // LANES + window_tiles(columns, devices) <= table.shape[1] // LANES
+            for d in range(devices)
+        )
+    )
+    return one_stream_each(*operands) if fits else many_per_stream(*operands)
+
+
 def solution(mesh):
     placed = (
         P("seq", "rep", None),

time: 418 us -> 104 us (0.25)
  the two profiles are of different devices: /device:TPU:9 before, /device:TPU:0 now
where the time goes in v1:
time: 104 us; the launch traced here: 103 us
  waiting for transfers between devices  55.4 us (53%)
  starting transfers between devices  23 us (22%)
  Pallas kernels  20.4 us (20%)
  local copies, waits for them, and re-layouts  2.96 us (3%)
    all_to_all x1, waiting for transfers between devices, one_stream_each(): got = lax.all_to_all(send, 'seq', split_axis=0, concat_axis=0, tiled=True)  44.3 us
    all_to_all x1, starting transfers between devices, one_stream_each(): lax.all_to_all(payload, 'seq', split_axis=0, concat_axis=0, tiled=True)  12.8 us
    all_to_all x1, waiting for transfers between devices, one_stream_each(): lax.all_to_all(payload, 'seq', split_axis=0, concat_axis=0, tiled=True)  8.97 us
    all_to_all x1, starting transfers between devices, one_stream_each(): got = lax.all_to_all(send, 'seq', split_axis=0, concat_axis=0, tiled=True)  7.52 us
    pallas_call x1, Pallas kernels, one_stream_each(): pl.pallas_call(functools.partial(attend_kernel, table_rows=table_rows), o...  5.81 us
    pallas_call x1, Pallas kernels, one_stream_each(): pl.pallas_call(select_kernel, out_shape=jax.ShapeDtypeStruct((REQUESTS, t...  5.63 us
    pallas_call x1, Pallas kernels, one_stream_each(): pl.pallas_call(functools.partial(prepare_kernel, devices=devices, columns...  5.39 us
    pallas_call x1, Pallas kernels, one_stream_each(): pl.pallas_call(functools.partial(finish_kernel, devices=devices, columns=...  3.59 us
  transfers between devices with their start and end apart: 4, of which 3 were waited for; matrix products, arithmetic and copies ran while one was open for 0% of the time, Pallas kernels for 6%

profile of v1, /device:TPU:0, one launch (start us, length us, event | category | flops | bytes accessed | tf_op | source)
XLA Modules:
  0.0 103.0 jit_solution(16280510968060714380)
XLA Ops:
  0.6 0.6 pad_add_fusion.place_ref
  1.2 5.4 %prepare.1 = (bf16[16,608,128]{2,1,0:T(8,128)(2,1)}, f32[80,80]{1,0:T(8,128)}) custom-call(s32[2]{0:T(128)} %pad_add_fusion.place_ref, bf16[2,16,5120]{2,1,0:T(8,128)(2,1)} %q_ref.1, bf16[2,16,5120]{2,1,0:T(8,128)(2,1)} %k_ref.1, bf16[2,16,5120]{2,1,0:T(8,128)(2,1)} %v_ref.1, bf16[2,16,5120]{2,1,0:T(8,128)(2,1)} %h_ref.1, bf16[64,5120]{1,0:T(8,128)(2,1)} %embed_ref.1, ...), custom_call_target="tpu_custom_call" | custom-call | tf_op jit(solution)/shard_map/prepare/pallas_call | solution.py:486
  6.6 0.0 copy-start.3
  6.6 7.5 %all-to-all-start = ((bf16[16,608,128]{2,1,0:T(8,128)(2,1)}), bf16[16,608,128]{2,1,0:T(8,128)(2,1)S(1)}, u32[]{:S(2)}, u32[]{:S(2)}) async-start(bf16[16,608,128]{2,1,0:T(8,128)(2,1)} %get-tuple-element.5), calls=%async_computation | async-start | bytes 4980736 | tf_op jit(solution)/shard_map/all_to_all | solution.py:509
  14.2 0.0 copy-done.3
  14.2 1.6 %collective-permute-start = (s32[8]{0:T(128)S(1)}, s32[8]{0:T(128)S(1)}, u32[]{:S(2)}, u32[]{:S(2)}) collective-permute-start(s32[8]{0:T(128)S(1)} %copy-done.3), channel_id=1, source_target_pairs={{0,16},{16,0},{1,17},{17,1},{2,18},{18,2},{3,19},{19,3},{4,20},{20... | collective-permute-start | bytes 104 | tf_op jit(solution)/shard_map/ppermute | solution.py:481
  15.7 2.0 %collective-permute-done.ids_ref = s32[8]{0:T(128)S(1)} collective-permute-done((s32[8]{0:T(128)S(1)}, s32[8]{0:T(128)S(1)}, u32[]{:S(2)}, u32[]{:S(2)}) %collective-permute-start) | collective-permute-done | bytes 64 | tf_op jit(solution)/shard_map/ppermute | solution.py:481
  17.8 0.0 copy-start.4
  17.8 44.3 %all-to-all-done.got_ref.table_ref.near_ref = bf16[16,608,128]{2,1,0:T(8,128)(2,1)S(1)} async-done(((bf16[16,608,128]{2,1,0:T(8,128)(2,1)}), bf16[16,608,128]{2,1,0:T(8,128)(2,1)S(1)}, u32[]{:S(2)}, u32[]{:S(2)}) %all-to-all-start) | async-done | bytes 2490400 | tf_op jit(solution)/shard_map/all_to_all | solution.py:509
  62.1 0.0 copy-done.4
  62.1 0.0 copy-start
  62.1 1.5 %copy-done = bf16[16,608,128]{2,1,0:T(8,128)(2,1)} copy-done((bf16[16,608,128]{2,1,0:T(8,128)(2,1)}, bf16[16,608,128]{2,1,0:T(8,128)(2,1)S(1)}, u32[]{:S(2)}) %copy-start) | copy-done | bytes 2490392
  63.6 5.6 %choose.1 = bf16[8,288,128]{2,1,0:T(8,128)(2,1)} custom-call(s32[8]{0:T(128)} %copy-done.4, bf16[16,608,128]{2,1,0:T(8,128)(2,1)} %copy-done), custom_call_target="tpu_custom_call" | custom-call | tf_op jit(solution)/shard_map/choose/pallas_call | solution.py:511
  69.2 0.0 copy-start.6
  69.2 0.0 copy-start.5
  69.2 1.2 %collective-permute-start.1 = (bf16[8,288,128]{2,1,0:T(8,128)(2,1)}, bf16[8,288,128]{2,1,0:T(8,128)(2,1)S(1)}, u32[]{:S(2)}, u32[]{:S(2)}) collective-permute-start(bf16[8,288,128]{2,1,0:T(8,128)(2,1)} %choose.1), channel_id=1, source_target_pairs={{0,16},{16,0},{1,17},{17,1},{2,18},{18,2},{3,19},{19,3},{4,20},{20... | collective-permute-start | bytes 1769480 | tf_op jit(solution)/shard_map/ppermute | solution.py:522
  70.4 5.8 %attend.1 = f32[16,24,128]{2,1,0:T(8,128)} custom-call(s32[2]{0:T(128)} %pad_add_fusion.place_ref, s32[8]{0:T(128)} %lengths_ref.1, bf16[16,608,128]{2,1,0:T(8,128)(2,1)} %copy-done, f32[16,5120]{1,0:T(8,128)} %gate_ref.1, f32[16,5120]{1,0:T(8,128)} %shift_ref.1, f32[16,5120]{1,0:T(8,128)} %scale_ref.1, bf16[64,5120]{1,0:T(8,128)(2,1)} %bitcast.14, ...), custom_call_target="tpu_custom_call" | custom-call | flops 1000000000 | bytes 4000000 | tf_op jit(solution)/shard_map/attend/pallas_call | solution.py:525
  76.2 12.8 %all-to-all-start.1 = ((f32[16,24,128]{2,1,0:T(8,128)}), f32[16,24,128]{2,1,0:T(8,128)S(1)}, u32[]{:S(2)}, u32[]{:S(2)}) async-start(f32[16,24,128]{2,1,0:T(8,128)} %attend.1), calls=%async_computation.1 | async-start | bytes 393216 | tf_op jit(solution)/shard_map/all_to_all | solution.py:550
  89.0 0.0 copy-done.6
  89.0 9.0 %all-to-all-done.1 = f32[16,24,128]{2,1,0:T(8,128)S(1)} async-done(((f32[16,24,128]{2,1,0:T(8,128)}), f32[16,24,128]{2,1,0:T(8,128)S(1)}, u32[]{:S(2)}, u32[]{:S(2)}) %all-to-all-start.1) | async-done | bytes 196640 | tf_op jit(solution)/shard_map/all_to_all | solution.py:550
  98.0 0.0 copy-start.1
  98.0 0.0 collective-permute-done.1.far_ref
  98.0 0.0 copy-start.2
  98.0 0.8 broadcast_in_dim.21.step_ref
  98.8 0.0 copy-done.5
  98.8 0.7 broadcast_in_dim.20.guidance_ref
  99.5 0.0 copy-done.1
  99.5 0.0 copy-done.2
  99.5 3.6 %finish.1 = (f32[2,8,64]{2,1,0:T(8,128)}, f32[2,8,64]{2,1,0:T(8,128)}, bf16[32,8,960]{2,1,0:T(8,128)(2,1)}) custom-call(s32[2]{0:T(128)} %pad_add_fusion.place_ref, s32[8]{0:T(128)} %ids_ref.1, f32[384,128]{1,0:T(8,128)} %bitcast.13, f32[8,128]{1,0:T(8,128)} %broadcast_in_dim.20.guidance_ref, f32[8,128]{1,0:T(8,128)} %broadcast_in_dim.21.step_ref, ...), custom_call_target="tpu_custom_call" | custom-call | tf_op jit(solution)/shard_map/finish/pallas_call | solution.py:555
  (1 shorter events, 0.0 us)
Async XLA Ops:
  6.6 7.5 %copy-start.3 = (s32[8]{0:T(128)S(1)}, s32[8]{0:T(128)}, u32[]{:S(2)}) copy-start(s32[8]{0:T(128)} %ids_ref.1) | copy-start | bytes 100
  6.6 55.5 %all-to-all-start = ((bf16[16,608,128]{2,1,0:T(8,128)(2,1)}), bf16[16,608,128]{2,1,0:T(8,128)(2,1)S(1)}, u32[]{:S(2)}, u32[]{:S(2)}) async-start(bf16[16,608,128]{2,1,0:T(8,128)(2,1)} %get-tuple-element.5), calls=%async_computation | async-start | bytes 4980736 | tf_op jit(solution)/shard_map/all_to_all | solution.py:509
  14.2 3.6 %collective-permute-start = (s32[8]{0:T(128)S(1)}, s32[8]{0:T(128)S(1)}, u32[]{:S(2)}, u32[]{:S(2)}) collective-permute-start(s32[8]{0:T(128)S(1)} %copy-done.3), channel_id=1, source_target_pairs={{0,16},{16,0},{1,17},{17,1},{2,18},{18,2},{3,19},{19,3},{4,20},{20... | collective-permute-start | bytes 104 | tf_op jit(solution)/shard_map/ppermute | solution.py:481
  17.8 44.3 %copy-start.4 = (s32[8]{0:T(128)}, s32[8]{0:T(128)S(1)}, u32[]{:S(2)}) copy-start(s32[8]{0:T(128)S(1)} %collective-permute-done.ids_ref) | copy-start | bytes 100
  62.1 1.5 %copy-start = (bf16[16,608,128]{2,1,0:T(8,128)(2,1)}, bf16[16,608,128]{2,1,0:T(8,128)(2,1)S(1)}, u32[]{:S(2)}) copy-start(bf16[16,608,128]{2,1,0:T(8,128)(2,1)S(1)} %all-to-all-done.got_ref.table_ref.near_ref) | copy-start | bytes 7471108
  69.2 19.8 %copy-start.6 = (s32[8]{0:T(128)S(1)}, s32[8]{0:T(128)}, u32[]{:S(2)}) copy-start(s32[8]{0:T(128)} %param.28) | copy-start | bytes 100
  69.2 29.6 %copy-start.5 = (f32[8]{0:T(128)S(1)}, f32[8]{0:T(128)}, u32[]{:S(2)}) copy-start(f32[8]{0:T(128)} %param.27) | copy-start | bytes 100
  69.2 28.8 %collective-permute-start.1 = (bf16[8,288,128]{2,1,0:T(8,128)(2,1)}, bf16[8,288,128]{2,1,0:T(8,128)(2,1)S(1)}, u32[]{:S(2)}, u32[]{:S(2)}) collective-permute-start(bf16[8,288,128]{2,1,0:T(8,128)(2,1)} %choose.1), channel_id=1, source_target_pairs={{0,16},{16,0},{1,17},{17,1},{2,18},{18,2},{3,19},{19,3},{4,20},{20... | collective-permute-start | bytes 1769480 | tf_op jit(solution)/shard_map/ppermute | solution.py:522
  76.2 21.8 %all-to-all-start.1 = ((f32[16,24,128]{2,1,0:T(8,128)}), f32[16,24,128]{2,1,0:T(8,128)S(1)}, u32[]{:S(2)}, u32[]{:S(2)}) async-start(f32[16,24,128]{2,1,0:T(8,128)} %attend.1), calls=%async_computation.1 | async-start | bytes 393216 | tf_op jit(solution)/shard_map/all_to_all | solution.py:550
  98.0 1.5 %copy-start.1 = (f32[16,24,128]{2,1,0:T(8,128)}, f32[16,24,128]{2,1,0:T(8,128)S(1)}, u32[]{:S(2)}) copy-start(f32[16,24,128]{2,1,0:T(8,128)S(1)} %all-to-all-done.1) | copy-start | bytes 589828
  98.0 1.5 %copy-start.2 = (bf16[8,288,128]{2,1,0:T(8,128)(2,1)}, bf16[8,288,128]{2,1,0:T(8,128)(2,1)S(1)}, u32[]{:S(2)}) copy-start(bf16[8,288,128]{2,1,0:T(8,128)(2,1)S(1)} %collective-permute-done.1.far_ref) | copy-start | bytes 1769476

commit v2 on v1

--- a/solution.py
+++ b/solution.py
@@ -14,7 +14,8 @@
 LANES = 128
 QUARTERS = 4
 TABLE_ROWS = 72
-VMEM_LIMIT = 56 << 20
+VMEM_LIMIT = 20 << 20
+PREPARE_VMEM_LIMIT = 56 << 20
 
 NT = (((1,), (1,)), ((), ()))
 
@@ -23,23 +24,15 @@
     return lax.dot_general(a, b, NT, preferred_element_type=jnp.float32)
 
 
-def prepare_kernel(
-    place_ref,
-    q_ref,
-    k_ref,
-    v_ref,
-    h_ref,
-    embed_ref,
-    bias_ref,
-    down_ref,
-    up_ref,
-    send_ref,
-    gram_ref,
-    *,
-    devices,
-    columns,
-    half_tiles,
-):
+def prepare_kernel(*refs, devices, columns, half_tiles):
+    sources, (send_ref, gram_ref), held, sems = refs[:8], refs[8:10], refs[10:18], refs[18]
+    copies = [
+        pltpu.make_async_copy(source, target, sems.at[index])
+        for index, (source, target) in enumerate(zip(sources, held))
+    ]
+    for copy in copies:
+        copy.start()
+    q_ref, k_ref, v_ref, h_ref, embed_ref, bias_ref, down_ref, up_ref = held
     row_count, stream_count, width = q_ref.shape
     quarter = width // QUARTERS
     tiles = quarter // LANES
@@ -50,6 +43,7 @@
     same = (to // 8 == at % stream_count) & (to % 8 == at // stream_count)
     permutation = jnp.where(same, 1.0, 0.0).astype(jnp.bfloat16)
     for kind, ref in enumerate((q_ref, k_ref, v_ref, h_ref)):
+        copies[kind].wait()
         stacked = jnp.concatenate(
             [
                 ref[token, :, part * quarter : (part + 1) * quarter]
@@ -66,6 +60,8 @@
                 :, tile * LANES : (tile + 1) * LANES
             ].reshape(stream_count, 8, LANES)
 
+    for copy in copies[4:7]:
+        copy.wait()
     bias = bias_ref[...]
     high = bias.astype(jnp.bfloat16).astype(jnp.float32)
     middle = (bias - high).astype(jnp.bfloat16).astype(jnp.float32)
@@ -90,7 +86,8 @@
     mixing = jnp.concatenate([mixing_high, mixing_low], axis=1)
 
     half = half_tiles * LANES
-    side = place_ref[1] * half
+    side = lax.axis_index("rep") * half
+    copies[7].wait()
     for target in range(devices):
         start = columns * target // LANES * LANES
         part = up_ref[:, pl.ds(pl.multiple_of(start + side, LANES), half)]
@@ -103,8 +100,20 @@
             ]
 
 
-def select_kernel(ids_ref, table_ref, out_ref):
-    out_ref[...] = table_ref[...]
+def choose_kernel(ids_ref, got_ref, out_ref, sems):
+    count = out_ref.shape[1]
+    copies = [
+        pltpu.make_async_copy(
+            got_ref.at[ids_ref[request], 0:count],
+            out_ref.at[request],
+            sems.at[request],
+        )
+        for request in range(REQUESTS)
+    ]
+    for copy in copies:
+        copy.start()
+    for copy in copies:
+        copy.wait()
 
 
 def group_sum(x):
@@ -114,14 +123,31 @@
     return grouped.reshape(x.shape)
 
 
+def modulate_kernel(gate_ref, shift_ref, scale_ref, weight_ref, rows_ref, head_ref):
+    width = gate_ref.shape[1]
+    quarter = width // QUARTERS
+    mine = lax.axis_index("seq")
+    part_of_row = lax.broadcasted_iota(jnp.int32, (8, quarter), 0) // 2
+    for index, ref in enumerate((gate_ref, shift_ref, scale_ref)):
+        block = ref[pl.ds(pl.multiple_of(mine // 8 * 8, 8), 8), :]
+        row = pltpu.roll(block, (8 - mine % 8) % 8, 0)[0:1]
+        value = jnp.zeros((8, quarter), jnp.float32)
+        for part in range(QUARTERS):
+            piece = row[:, part * quarter : (part + 1) * quarter]
+            value = jnp.where(part_of_row == part, jnp.broadcast_to(piece, value.shape), value)
+        rows_ref[index] = value
+    channels = weight_ref.shape[0]
+    for part in range(QUARTERS):
+        head_ref[part * channels : (part + 1) * channels, :] = weight_ref[
+            :, part * quarter : (part + 1) * quarter
+        ]
+
+
 def attend_kernel(
-    place_ref,
     lengths_ref,
     got_ref,
-    gate_ref,
-    shift_ref,
-    scale_ref,
-    weight_ref,
+    rows_ref,
+    head_ref,
     bias_ref,
     latent_ref,
     out_ref,
@@ -131,35 +157,20 @@
     table_rows,
 ):
     devices = got_ref.shape[0]
-    width = gate_ref.shape[1]
-    quarter = width // QUARTERS
+    quarter = rows_ref.shape[2]
+    width = quarter * QUARTERS
     tiles = quarter // LANES
     size = devices * 8
-    mine = place_ref[0]
-    limit = lengths_ref[mine % REQUESTS]
+    limit = lengths_ref[lax.axis_index("seq") % REQUESTS]
     score_scale = 1.0 / HEAD_DIM**0.5
 
     row = lax.broadcasted_iota(jnp.int32, (size, size), 0)
     column = lax.broadcasted_iota(jnp.int32, (size, size), 1)
     key_token = column // 8 * 2 + column % 2
     allowed = (row % 8 // 2 == column % 8 // 2) & (key_token < limit)
-    part_of_row = lax.broadcasted_iota(jnp.int32, (8, LANES), 0) // 2
-
-    def own_row(ref):
-        block = ref[pl.ds(pl.multiple_of(mine // 8 * 8, 8), 8), :]
-        return pltpu.roll(block, (8 - mine % 8) % 8, 0)[0:1]
-
-    gate, shift, scale = own_row(gate_ref), own_row(shift_ref), own_row(scale_ref)
-
-    def per_row(values, tile):
-        value = jnp.zeros((8, LANES), jnp.float32)
-        for part in range(QUARTERS):
-            first = part * quarter + tile * LANES
-            piece = values[:, first : first + LANES]
-            value = jnp.where(part_of_row == part, jnp.broadcast_to(piece, (8, LANES)), value)
-        return value
-
-    def widened(value):
+
+    def modulation(index, tile):
+        value = rows_ref[index, :, tile * LANES : (tile + 1) * LANES]
         return jnp.broadcast_to(value[None], (devices, 8, LANES)).reshape(size, LANES)
 
     total = jnp.zeros((size, LANES), jnp.float32)
@@ -179,9 +190,7 @@
         attended = jnp.dot(
             weights.astype(jnp.bfloat16), v, preferred_element_type=jnp.float32
         ).astype(jnp.bfloat16)
-        residual = h.astype(jnp.float32) + widened(per_row(gate, tile)) * attended.astype(
-            jnp.float32
-        )
+        residual = h.astype(jnp.float32) + modulation(0, tile) * attended.astype(jnp.float32)
         residual_ref[tile] = residual
         total = total + residual
     mean = jnp.sum(group_sum(total), axis=-1, keepdims=True) * (1.0 / width)
@@ -192,20 +201,13 @@
         total = total + centered * centered
     variance = jnp.sum(group_sum(total), axis=-1, keepdims=True) * (1.0 / width)
     inverse = lax.rsqrt(variance + 1e-06)
-    channels = weight_ref.shape[0]
+    channels = head_ref.shape[0] // QUARTERS
     product = jnp.zeros((size, QUARTERS * channels), jnp.float32)
     for tile in range(tiles):
-        normed = residual_ref[tile] * inverse * widened(
-            1.0 + per_row(scale, tile)
-        ) + widened(per_row(shift, tile))
-        weight = jnp.concatenate(
-            [
-                weight_ref[:, part * quarter + tile * LANES : part * quarter + (tile + 1) * LANES]
-                for part in range(QUARTERS)
-            ],
-            axis=0,
+        normed = residual_ref[tile] * inverse * (1.0 + modulation(2, tile)) + modulation(1, tile)
+        product = product + nt_dot(
+            normed.astype(jnp.bfloat16), head_ref[:, tile * LANES : (tile + 1) * LANES]
         )
-        product = product + nt_dot(normed.astype(jnp.bfloat16), weight)
     row = lax.broadcasted_iota(jnp.int32, product.shape, 0)
     column = lax.broadcasted_iota(jnp.int32, product.shape, 1)
     product = jnp.where(row % 8 // 2 == column // channels, product, 0.0)
@@ -224,7 +226,6 @@
 
 
 def finish_kernel(
-    place_ref,
     ids_ref,
     got_ref,
     guidance_ref,
@@ -244,8 +245,14 @@
     half_tiles,
 ):
     block = devices + REQUESTS
-    guidance = guidance_ref[...]
-    step = step_ref[...]
+    request_row = lax.broadcasted_iota(jnp.int32, (REQUESTS, LANES), 0)
+    guidance = jnp.zeros((REQUESTS, LANES), jnp.float32)
+    position = jnp.zeros((REQUESTS, LANES), jnp.int32)
+    for request in range(REQUESTS):
+        guidance = jnp.where(request_row == request, guidance_ref[request], guidance)
+        position = jnp.where(request_row == request, step_ref[request], position)
+    sigma_now = noise_level(position.astype(jnp.float32))
+    step = noise_level((position + 1).astype(jnp.float32)) - sigma_now
     lane = lax.broadcasted_iota(jnp.int32, (REQUESTS, LANES), 1)
     channels = LANES // 2
     pieces = []
@@ -260,7 +267,7 @@
         tail = jnp.where(lane < channels + 3, 1.0, 0.0)
         pieces.append(jnp.where(lane < channels, latent_next, tail))
         pieces.append(jnp.where(lane < channels, pltpu.roll(latent_next, channels, 1), tail))
-    mine = place_ref[0]
+    mine = lax.axis_index("seq")
     velocity = velocity_all[mine]
     latent_next = latent_all[mine]
     velocity_ref[0] = velocity[:, :channels]
@@ -290,17 +297,18 @@
         axis=1,
     ).astype(jnp.bfloat16)
     half = half_tiles * LANES
-    side = place_ref[1]
-    for which, take in (
-        (side, lambda request: near_ref[ids_ref[request]]),
-        (1 - side, lambda request: far_ref[request]),
-    ):
-        tables = [take(request) for request in range(REQUESTS)]
+    side = lax.axis_index("rep")
+
+    def near(request, tile):
+        return near_ref[ids_ref[request], tile * TABLE_ROWS : (tile + 1) * TABLE_ROWS, :]
+
+    def far(request, tile):
+        return far_ref[request, tile * TABLE_ROWS : (tile + 1) * TABLE_ROWS, :]
+
+    for which, take in ((side, near), (1 - side, far)):
         right = jnp.concatenate(
             [
-                jnp.concatenate(
-                    [table[tile * TABLE_ROWS : (tile + 1) * TABLE_ROWS] for table in tables], axis=0
-                )
+                jnp.concatenate([take(request, tile) for request in range(REQUESTS)], axis=0)
                 for tile in range(half_tiles)
             ],
             axis=1,
@@ -476,13 +484,23 @@
     half_tiles = window_tiles(columns, devices) // 2
     table_rows = half_tiles * TABLE_ROWS
     send_rows = table_rows + 4 * (width // QUARTERS // LANES) * 8
-    place = jnp.stack([lax.axis_index("seq"), lax.axis_index("rep")]).astype(jnp.int32)
     swap = [(0, 1), (1, 0)]
     other_ids = lax.ppermute(adapter_ids, "rep", swap)
     smem = pl.BlockSpec(memory_space=pltpu.SMEM)
     vmem = pl.BlockSpec(memory_space=pltpu.VMEM)
+    anywhere = pl.BlockSpec(memory_space=pl.ANY)
     params = pltpu.CompilerParams(vmem_limit_bytes=VMEM_LIMIT)
 
+    sources = (
+        queries,
+        key_states,
+        value_states,
+        hidden,
+        embed_weight,
+        embed_bias[None, :],
+        adapter_down[0].T,
+        adapter_up[0].T,
+    )
     send, gram = pl.pallas_call(
         functools.partial(
             prepare_kernel, devices=devices, columns=columns, half_tiles=half_tiles
@@ -491,44 +509,47 @@
             jax.ShapeDtypeStruct((devices, send_rows, LANES), jnp.bfloat16),
             jax.ShapeDtypeStruct((80, 80), jnp.float32),
         ),
-        in_specs=[smem] + [vmem] * 8,
+        in_specs=[anywhere] * len(sources),
         out_specs=(vmem, vmem),
+        scratch_shapes=[pltpu.VMEM(source.shape, source.dtype) for source in sources]
+        + [pltpu.SemaphoreType.DMA((len(sources),))],
+        compiler_params=pltpu.CompilerParams(vmem_limit_bytes=PREPARE_VMEM_LIMIT),
+        name="prepare",
+    )(*sources)
+    got = lax.all_to_all(send, "seq", split_axis=0, concat_axis=0, tiled=True)
+
+    chosen = pl.pallas_call(
+        choose_kernel,
+        out_shape=jax.ShapeDtypeStruct((REQUESTS, table_rows, LANES), jnp.bfloat16),
+        in_specs=[smem, anywhere],
+        out_specs=anywhere,
+        scratch_shapes=[pltpu.SemaphoreType.DMA((REQUESTS,))],
         compiler_params=params,
-        name="prepare",
-    )(
-        place,
-        queries,
-        key_states,
-        value_states,
-        hidden,
-        embed_weight,
-        embed_bias[None, :],
-        adapter_down[0].T,
-        adapter_up[0].T,
-    )
-    got = lax.all_to_all(send, "seq", split_axis=0, concat_axis=0, tiled=True)
-
-    chosen = pl.pallas_call(
-        select_kernel,
-        out_shape=jax.ShapeDtypeStruct((REQUESTS, table_rows, LANES), jnp.bfloat16),
-        grid_spec=pltpu.PrefetchScalarGridSpec(
-            num_scalar_prefetch=1,
-            grid=(REQUESTS,),
-            in_specs=[pl.BlockSpec((1, table_rows, LANES), lambda r, ids: (ids[r], 0, 0))],
-            out_specs=pl.BlockSpec((1, table_rows, LANES), lambda r, ids: (r, 0, 0)),
-        ),
         name="choose",
     )(other_ids, got)
     far = lax.ppermute(chosen, "rep", swap)
 
+    quarter = width // QUARTERS
+    channels = head_weight.shape[1]
+    rows, head = pl.pallas_call(
+        modulate_kernel,
+        out_shape=(
+            jax.ShapeDtypeStruct((3, 8, quarter), jnp.float32),
+            jax.ShapeDtypeStruct((QUARTERS * channels, quarter), head_weight.dtype),
+        ),
+        in_specs=[vmem] * 4,
+        out_specs=(vmem, vmem),
+        compiler_params=params,
+        name="modulate",
+    )(residual_gate, head_shift, head_scale, head_weight.T)
     payload_rows = devices + REQUESTS
     payload = pl.pallas_call(
         functools.partial(attend_kernel, table_rows=table_rows),
         out_shape=jax.ShapeDtypeStruct((devices, payload_rows, LANES), jnp.float32),
-        in_specs=[smem, smem] + [vmem] * 7,
+        in_specs=[smem] + [vmem] * 5,
         out_specs=vmem,
         scratch_shapes=[
-            pltpu.VMEM((width // QUARTERS // LANES, devices * 8, LANES), jnp.float32),
+            pltpu.VMEM((quarter // LANES, devices * 8, LANES), jnp.float32),
             pltpu.VMEM((devices * 8, LANES), jnp.float32),
         ],
         compiler_params=params,
@@ -537,20 +558,15 @@
             flops=10**9, bytes_accessed=4 * 10**6, transcendentals=2 * 10**5
         ),
     )(
-        place,
         lengths,
         got,
-        residual_gate,
-        head_shift,
-        head_scale,
-        head_weight.T,
+        rows,
+        head,
         head_bias[None, :],
         latent,
     )
     shared = lax.all_to_all(payload, "seq", split_axis=0, concat_axis=0, tiled=True)
 
-    sigma_now = noise_level(step_index.astype(jnp.float32))
-    sigma_next = noise_level((step_index + 1).astype(jnp.float32))
     across = (REQUESTS, LANES)
     return pl.pallas_call(
         functools.partial(finish_kernel, devices=devices, columns=columns, half_tiles=half_tiles),
@@ -559,7 +575,7 @@
             jax.ShapeDtypeStruct(latent.shape, jnp.float32),
             jax.ShapeDtypeStruct((row_count * devices, REQUESTS, columns), jnp.bfloat16),
         ),
-        in_specs=[smem, smem] + [vmem] * 6,
+        in_specs=[smem, vmem, smem, smem] + [vmem] * 3,
         out_specs=(vmem, vmem, vmem),
         scratch_shapes=[
             pltpu.VMEM((devices,) + across, jnp.float32),
@@ -569,11 +585,10 @@
         compiler_params=params,
         name="finish",
     )(
-        place,
         adapter_ids,
         shared.reshape(devices * payload_rows, LANES),
-        jnp.broadcast_to(guidance[:, None], across),
-        jnp.broadcast_to((sigma_next - sigma_now)[:, None], across),
+        guidance,
+        step_index,
         gram,
         got,
         far,

time: 104 us -> 91.5 us (0.88)
  blocking collectives: 0 us -> 21.6 us
  starting transfers between devices: 23 us -> 10.5 us
  waiting for transfers between devices: 55.4 us -> 46.3 us
  Pallas kernels: 20.4 us -> 12 us
  local copies, waits for them, and re-layouts: 2.96 us -> 0.06 us
    all_to_all x0 -> x1, blocking collectives: none -> 21.6 us  [one_stream_each(): lax.all_to_all(payload, 'seq', split_axis=0, concat_axis=0, tiled=True)]
    all_to_all x1 -> x0, starting transfers between devices: 12.8 us -> none  [one_stream_each(): lax.all_to_all(payload, 'seq', split_axis=0, concat_axis=0, tiled=True)]
    all_to_all x1 -> x0, waiting for transfers between devices: 8.97 us -> none  [one_stream_each(): lax.all_to_all(payload, 'seq', split_axis=0, concat_axis=0, tiled=True)]
    pallas_call x1 -> x2, Pallas kernels: 5.63 us -> 1.48 us  [the longest x1 1.39 us: one_stream_each(): pl.pallas_call(choose_kernel, out_shape=jax.ShapeDtypeStruct((REQUESTS, t...]
    pallas_call x1, Pallas kernels: 5.81 us -> 3.51 us  [one_stream_each(): pl.pallas_call(functools.partial(attend_kernel, table_rows=table_rows), o...]
    broadcast_in_dim x2 -> x0, local copies, waits for them, and re-layouts: 1.46 us -> none  [the longest x1 0.8 us: one_stream_each(): jnp.broadcast_to((sigma_next - sigma_now)[:, None], across)]
    unnamed x14 -> x22, local copies, waits for them, and re-layouts: 1.49 us -> 0.06 us
    pallas_call x1, Pallas kernels: 3.59 us -> 2.21 us  [one_stream_each(): pl.pallas_call(functools.partial(finish_kernel, devices=devices, columns=...]
  transfers between devices with their start and end apart: 4 -> 3, of which waited for: 3 -> 2; matrix products, arithmetic and copies ran while one was open for 0% -> 0% of each run, Pallas kernels for 6% -> 4%
where the time goes in v2:
time: 91.5 us; the launch traced here: 91.3 us
  waiting for transfers between devices  46.3 us (51%)
  blocking collectives  21.6 us (24%)
  Pallas kernels  12 us (13%)
  starting transfers between devices  10.5 us (11%)
    all_to_all x1, waiting for transfers between devices, one_stream_each(): got = lax.all_to_all(send, 'seq', split_axis=0, concat_axis=0, tiled=True)  44.3 us
    all_to_all x1, blocking collectives, one_stream_each(): lax.all_to_all(payload, 'seq', split_axis=0, concat_axis=0, tiled=True)  21.6 us
    all_to_all x1, starting transfers between devices, one_stream_each(): got = lax.all_to_all(send, 'seq', split_axis=0, concat_axis=0, tiled=True)  7.4 us
    pallas_call x1, Pallas kernels, one_stream_each(): pl.pallas_call(functools.partial(prepare_kernel, devices=devices, columns...  4.78 us
    pallas_call x1, Pallas kernels, one_stream_each(): pl.pallas_call(functools.partial(attend_kernel, table_rows=table_rows), o...  3.51 us
    pallas_call x1, Pallas kernels, one_stream_each(): pl.pallas_call(functools.partial(finish_kernel, devices=devices, columns=...  2.21 us
    ppermute x1, waiting for transfers between devices, one_stream_each(): other_ids = lax.ppermute(adapter_ids, 'rep', swap)  2.05 us
  transfers between devices with their start and end apart: 3, of which 2 were waited for; matrix products, arithmetic and copies ran while one was open for 0% of the time, Pallas kernels for 4%

profile of v2, /device:TPU:0, one launch (start us, length us, event | category | flops | bytes accessed | tf_op | source)
XLA Modules:
  0.0 91.3 jit_solution(8613732363094385470)
XLA Ops:
  0.6 4.8 %prepare.1 = (bf16[16,608,128]{2,1,0:T(8,128)(2,1)}, f32[80,80]{1,0:T(8,128)}) custom-call(bf16[2,16,5120]{2,1,0:T(8,128)(2,1)} %refs_0_.1, bf16[2,16,5120]{2,1,0:T(8,128)(2,1)} %refs_1_.1, bf16[2,16,5120]{2,1,0:T(8,128)(2,1)} %refs_2_.1, bf16[2,16,5120]{2,1,0:T(8,128)(2,1)} %refs_3_.1, bf16[64,5120]{1,0:T(8,128)(2,1)} %refs_4_.1, f32[1,5120]{1,0:T(1,128)} %bitcast.15, ...), custom_call_target="tpu_custom_call" | custom-call | tf_op jit(solution)/shard_map/prepare/pallas_call | solution.py:504
  5.4 0.0 copy-start.5
  5.4 7.4 %all-to-all-start = ((bf16[16,608,128]{2,1,0:T(8,128)(2,1)}), bf16[16,608,128]{2,1,0:T(8,128)(2,1)S(1)}, u32[]{:S(2)}, u32[]{:S(2)}) async-start(bf16[16,608,128]{2,1,0:T(8,128)(2,1)} %get-tuple-element.7), calls=%async_computation | async-start | bytes 4980736 | tf_op jit(solution)/shard_map/all_to_all | solution.py:519
  12.8 0.0 copy-done.5
  12.8 0.0 copy-start
  12.9 0.0 copy-start.1
  12.9 0.0 copy-start.8
  12.9 0.0 copy-start.9
  12.9 0.0 copy-start.10
  12.9 1.6 %collective-permute-start = (s32[8]{0:T(128)S(1)}, s32[8]{0:T(128)S(1)}, u32[]{:S(2)}, u32[]{:S(2)}) collective-permute-start(s32[8]{0:T(128)S(1)} %copy-done.5), channel_id=1, source_target_pairs={{0,16},{16,0},{1,17},{17,1},{2,18},{18,2},{3,19},{19,3},{4,20},{20... | collective-permute-start | bytes 104 | tf_op jit(solution)/shard_map/ppermute | solution.py:488
  14.5 2.1 %collective-permute-done.ids_ref = s32[8]{0:T(128)S(1)} collective-permute-done((s32[8]{0:T(128)S(1)}, s32[8]{0:T(128)S(1)}, u32[]{:S(2)}, u32[]{:S(2)}) %collective-permute-start) | collective-permute-done | bytes 64 | tf_op jit(solution)/shard_map/ppermute | solution.py:488
  16.5 44.3 %all-to-all-done.got_ref.near_ref = bf16[16,608,128]{2,1,0:T(8,128)(2,1)S(1)} async-done(((bf16[16,608,128]{2,1,0:T(8,128)(2,1)}), bf16[16,608,128]{2,1,0:T(8,128)(2,1)S(1)}, u32[]{:S(2)}, u32[]{:S(2)}) %all-to-all-start) | async-done | bytes 2490400 | tf_op jit(solution)/shard_map/all_to_all | solution.py:519
  60.8 0.0 copy-start.2
  60.8 0.0 copy-start.3
  60.8 1.4 %choose.1 = bf16[8,288,128]{2,1,0:T(8,128)(2,1)S(1)} custom-call(s32[8]{0:T(128)S(1)} %collective-permute-done.ids_ref, bf16[16,608,128]{2,1,0:T(8,128)(2,1)S(1)} %all-to-all-done.got_ref.near_ref), custom_call_target="tpu_custom_call" | custom-call | tf_op jit(solution)/shard_map/choose/pallas_call | solution.py:521
  62.2 1.6 %collective-permute-start.1 = (bf16[8,288,128]{2,1,0:T(8,128)(2,1)S(1)}, bf16[8,288,128]{2,1,0:T(8,128)(2,1)S(1)}, u32[]{:S(2)}, u32[]{:S(2)}) collective-permute-start(bf16[8,288,128]{2,1,0:T(8,128)(2,1)S(1)} %choose.1), channel_id=1, source_target_pairs={{0,16},{16,0},{1,17},{17,1},{2,18},{18,2},{3,19},{19,3},{4,20},{20... | collective-permute-start | bytes 1769480 | tf_op jit(solution)/shard_map/ppermute | solution.py:530
  63.8 0.0 copy-done
  63.8 0.0 copy-done.1
  63.8 0.0 copy-done.2
  63.8 0.0 copy-done.3
  63.8 0.0 copy-start.4
  63.8 0.0 copy-start.6
  63.8 0.0 copy-start.7
  63.8 0.1 modulate.1
  63.9 0.0 copy-done.8
  63.9 0.0 copy-done.9
  63.9 0.0 copy-done.10
  63.9 3.5 %attend.1 = f32[16,24,128]{2,1,0:T(8,128)S(1)} custom-call(s32[8]{0:T(128)S(1)} %copy-done.9, bf16[16,608,128]{2,1,0:T(8,128)(2,1)S(1)} %all-to-all-done.got_ref.near_ref, f32[3,8,1280]{2,1,0:T(8,128)S(1)} %get-tuple-element.8.rows_ref, bf16[256,1280]{1,0:T(8,128)(2,1)S(1)} %get-tuple-element.9.head_ref, f32[1,64]{1,0:T(1,128)S(1)} %bitcast.12, ...), custom_call_target="tpu_custom_call" | custom-call | flops 1000000000 | bytes 4000000 | tf_op jit(solution)/shard_map/attend/pallas_call | solution.py:546
  67.4 21.6 %all_to_all.10 = f32[16,24,128]{2,1,0:T(8,128)S(1)} all-to-all(f32[16,24,128]{2,1,0:T(8,128)S(1)} %attend.1), channel_id=1, replica_groups=mesh['rep'=2,'seq'=16] {'seq'}, dimensions={0} | all-to-all | bytes 393216 | tf_op jit(solution)/shard_map/all_to_all | solution.py:568
  89.0 0.0 collective-permute-done.1.far_ref
  89.0 0.0 copy-done.4
  89.0 0.0 copy-done.6
  89.0 0.0 copy-done.7
  89.0 2.2 %finish.1 = (f32[2,8,64]{2,1,0:T(8,128)}, f32[2,8,64]{2,1,0:T(8,128)}, bf16[32,8,960]{2,1,0:T(8,128)(2,1)}) custom-call(s32[8]{0:T(128)S(1)} %copy-done.5, f32[384,128]{1,0:T(8,128)S(1)} %bitcast.10, f32[8]{0:T(128)S(1)} %copy-done.6, s32[8]{0:T(128)S(1)} %copy-done.7, f32[80,80]{1,0:T(8,128)S(1)} %copy-done.4, ...), custom_call_target="tpu_custom_call" | custom-call | tf_op jit(solution)/shard_map/finish/pallas_call | solution.py:571
Async XLA Ops:
  5.4 7.4 %copy-start.5 = (s32[8]{0:T(128)S(1)}, s32[8]{0:T(128)}, u32[]{:S(2)}) copy-start(s32[8]{0:T(128)} %ids_ref.1) | copy-start | bytes 100
  5.4 55.4 %all-to-all-start = ((bf16[16,608,128]{2,1,0:T(8,128)(2,1)}), bf16[16,608,128]{2,1,0:T(8,128)(2,1)S(1)}, u32[]{:S(2)}, u32[]{:S(2)}) async-start(bf16[16,608,128]{2,1,0:T(8,128)(2,1)} %get-tuple-element.7), calls=%async_computation | async-start | bytes 4980736 | tf_op jit(solution)/shard_map/all_to_all | solution.py:519
  12.8 50.9 %copy-start = (bf16[5120,64]{0,1:T(8,128)(2,1)S(1)}, bf16[5120,64]{0,1:T(8,128)(2,1)}, u32[]{:S(2)}) copy-start(bf16[5120,64]{0,1:T(8,128)(2,1)} %param.25) | copy-start | bytes 1966084
  12.9 50.9 %copy-start.1 = (f32[16,5120]{1,0:T(8,128)S(1)}, f32[16,5120]{1,0:T(8,128)}, u32[]{:S(2)}) copy-start(f32[16,5120]{1,0:T(8,128)} %gate_ref.1) | copy-start | bytes 983044
  12.9 51.0 %copy-start.8 = (f32[2,8,64]{2,1,0:T(8,128)S(1)}, f32[2,8,64]{2,1,0:T(8,128)}, u32[]{:S(2)}) copy-start(f32[2,8,64]{2,1,0:T(8,128)} %latent_ref.1) | copy-start | bytes 12292
  12.9 51.0 %copy-start.9 = (s32[8]{0:T(128)S(1)}, s32[8]{0:T(128)}, u32[]{:S(2)}) copy-start(s32[8]{0:T(128)} %lengths_ref.1) | copy-start | bytes 100
  12.9 51.0 %copy-start.10 = (f32[64]{0:T(128)S(1)}, f32[64]{0:T(128)}, u32[]{:S(2)}) copy-start(f32[64]{0:T(128)} %param.26) | copy-start | bytes 772
  12.9 3.6 %collective-permute-start = (s32[8]{0:T(128)S(1)}, s32[8]{0:T(128)S(1)}, u32[]{:S(2)}, u32[]{:S(2)}) collective-permute-start(s32[8]{0:T(128)S(1)} %copy-done.5), channel_id=1, source_target_pairs={{0,16},{16,0},{1,17},{17,1},{2,18},{18,2},{3,19},{19,3},{4,20},{20... | collective-permute-start | bytes 104 | tf_op jit(solution)/shard_map/ppermute | solution.py:488
  60.8 3.0 %copy-start.2 = (f32[16,5120]{1,0:T(8,128)S(1)}, f32[16,5120]{1,0:T(8,128)}, u32[]{:S(2)}) copy-start(f32[16,5120]{1,0:T(8,128)} %shift_ref.1) | copy-start | bytes 983044
  60.8 3.0 %copy-start.3 = (f32[16,5120]{1,0:T(8,128)S(1)}, f32[16,5120]{1,0:T(8,128)}, u32[]{:S(2)}) copy-start(f32[16,5120]{1,0:T(8,128)} %scale_ref.1) | copy-start | bytes 983044
  62.2 26.8 %collective-permute-start.1 = (bf16[8,288,128]{2,1,0:T(8,128)(2,1)S(1)}, bf16[8,288,128]{2,1,0:T(8,128)(2,1)S(1)}, u32[]{:S(2)}, u32[]{:S(2)}) collective-permute-start(bf16[8,288,128]{2,1,0:T(8,128)(2,1)S(1)} %choose.1), channel_id=1, source_target_pairs={{0,16},{16,0},{1,17},{17,1},{2,18},{18,2},{3,19},{19,3},{4,20},{20... | collective-permute-start | bytes 1769480 | tf_op jit(solution)/shard_map/ppermute | solution.py:530
  63.8 25.3 %copy-start.4 = (f32[80,80]{1,0:T(8,128)S(1)}, f32[80,80]{1,0:T(8,128)}, u32[]{:S(2)}) copy-start(f32[80,80]{1,0:T(8,128)} %get-tuple-element.10.gram_ref) | copy-start | bytes 76804
  63.8 25.3 %copy-start.6 = (f32[8]{0:T(128)S(1)}, f32[8]{0:T(128)}, u32[]{:S(2)}) copy-start(f32[8]{0:T(128)} %guidance_ref.1) | copy-start | bytes 100
  63.8 25.2 %copy-start.7 = (s32[8]{0:T(128)S(1)}, s32[8]{0:T(128)}, u32[]{:S(2)}) copy-start(s32[8]{0:T(128)} %step_ref.1) | copy-start | bytes 100

commit v3 on v2

--- a/solution.py
+++ b/solution.py
@@ -13,7 +13,8 @@
 STEPS = 10
 LANES = 128
 QUARTERS = 4
-TABLE_ROWS = 72
+TABLE_ROWS = 64
+BIAS_ROWS = 8
 VMEM_LIMIT = 20 << 20
 PREPARE_VMEM_LIMIT = 56 << 20
 
@@ -25,7 +26,8 @@
 
 
 def prepare_kernel(*refs, devices, columns, half_tiles):
-    sources, (send_ref, gram_ref), held, sems = refs[:8], refs[8:10], refs[10:18], refs[18]
+    sources, (sent_ref, gram_ref), held = refs[:8], refs[8:10], refs[10:18]
+    send_ref, sems, out_sems = refs[18:]
     copies = [
         pltpu.make_async_copy(source, target, sems.at[index])
         for index, (source, target) in enumerate(zip(sources, held))
@@ -36,7 +38,7 @@
     row_count, stream_count, width = q_ref.shape
     quarter = width // QUARTERS
     tiles = quarter // LANES
-    table_rows = half_tiles * TABLE_ROWS
+    table_rows = half_tiles * TABLE_ROWS + BIAS_ROWS
     size = stream_count * 8
     to = lax.broadcasted_iota(jnp.int32, (size, size), 0)
     at = lax.broadcasted_iota(jnp.int32, (size, size), 1)
@@ -59,6 +61,13 @@
             send_ref[:, first : first + 8, :] = moved[
                 :, tile * LANES : (tile + 1) * LANES
             ].reshape(stream_count, 8, LANES)
+
+    writes = [
+        pltpu.make_async_copy(
+            send_ref.at[:, table_rows:], sent_ref.at[:, table_rows:], out_sems.at[0]
+        )
+    ]
+    writes[0].start()
 
     for copy in copies[4:7]:
         copy.wait()
@@ -88,16 +97,35 @@
     half = half_tiles * LANES
     side = lax.axis_index("rep") * half
     copies[7].wait()
+    row = lax.broadcasted_iota(jnp.int32, (BIAS_ROWS, LANES), 0)
     for target in range(devices):
         start = columns * target // LANES * LANES
         part = up_ref[:, pl.ds(pl.multiple_of(start + side, LANES), half)]
         table = jnp.dot(
             mixing, jnp.concatenate([part, part], axis=0), preferred_element_type=jnp.float32
-        ).astype(jnp.bfloat16)
+        )
+        biases = jnp.zeros((BIAS_ROWS, LANES), jnp.float32)
         for tile in range(half_tiles):
-            send_ref[target, tile * TABLE_ROWS : (tile + 1) * TABLE_ROWS, :] = table[
-                :, tile * LANES : (tile + 1) * LANES
-            ]
+            piece = table[:, tile * LANES : (tile + 1) * LANES]
+            send_ref[target, tile * TABLE_ROWS : (tile + 1) * TABLE_ROWS, :] = piece[
+                :TABLE_ROWS
+            ].astype(jnp.bfloat16)
+            biases = jnp.where(
+                row == tile,
+                jnp.broadcast_to(piece[TABLE_ROWS : TABLE_ROWS + 1], biases.shape),
+                biases,
+            )
+        send_ref[target, half_tiles * TABLE_ROWS : table_rows, :] = biases.astype(jnp.bfloat16)
+        writes.append(
+            pltpu.make_async_copy(
+                send_ref.at[target, 0:table_rows],
+                sent_ref.at[target, 0:table_rows],
+                out_sems.at[1 + target],
+            )
+        )
+        writes[-1].start()
+    for write in writes:
+        write.wait()
 
 
 def choose_kernel(ids_ref, got_ref, out_ref, sems):
@@ -299,22 +327,41 @@
     half = half_tiles * LANES
     side = lax.axis_index("rep")
 
-    def near(request, tile):
-        return near_ref[ids_ref[request], tile * TABLE_ROWS : (tile + 1) * TABLE_ROWS, :]
-
-    def far(request, tile):
-        return far_ref[request, tile * TABLE_ROWS : (tile + 1) * TABLE_ROWS, :]
-
+    def near(request, first, last):
+        return near_ref[ids_ref[request], first:last, :]
+
+    def far(request, first, last):
+        return far_ref[request, first:last, :]
+
+    bias_row = lax.broadcasted_iota(jnp.int32, (REQUESTS, LANES), 0)
+    bias_at = half_tiles * TABLE_ROWS
     for which, take in ((side, near), (1 - side, far)):
         right = jnp.concatenate(
             [
-                jnp.concatenate([take(request, tile) for request in range(REQUESTS)], axis=0)
+                jnp.concatenate(
+                    [
+                        take(request, tile * TABLE_ROWS, (tile + 1) * TABLE_ROWS)
+                        for request in range(REQUESTS)
+                    ],
+                    axis=0,
+                )
                 for tile in range(half_tiles)
             ],
             axis=1,
         )
-        product = jnp.dot(left, right, preferred_element_type=jnp.float32) * inverse
-        product_ref[:, pl.ds(pl.multiple_of(which * half, LANES), half)] = product
+        biases = [jnp.zeros((REQUESTS, LANES), jnp.float32)] * half_tiles
+        for request in range(REQUESTS):
+            block = take(request, bias_at, bias_at + BIAS_ROWS).astype(jnp.float32)
+            biases = [
+                jnp.where(bias_row == request, jnp.broadcast_to(block[t : t + 1], bias.shape), bias)
+                for t, bias in enumerate(biases)
+            ]
+        bias = jnp.concatenate(biases, axis=1)
+        product = jnp.dot(left, right, preferred_element_type=jnp.float32)
+        product = product.reshape(rows // REQUESTS, REQUESTS, half) + bias[None]
+        product_ref[:, pl.ds(pl.multiple_of(which * half, LANES), half)] = (
+            product.reshape(rows, half) * inverse
+        )
     shape = delta_ref.shape
     offsets = sorted({columns * target % LANES for target in range(devices)})
     own = columns * mine % LANES
@@ -482,7 +529,7 @@
     row_count, stream_count, width = queries.shape
     columns = adapter_up.shape[1] // devices
     half_tiles = window_tiles(columns, devices) // 2
-    table_rows = half_tiles * TABLE_ROWS
+    table_rows = half_tiles * TABLE_ROWS + BIAS_ROWS
     send_rows = table_rows + 4 * (width // QUARTERS // LANES) * 8
     swap = [(0, 1), (1, 0)]
     other_ids = lax.ppermute(adapter_ids, "rep", swap)
@@ -510,9 +557,13 @@
             jax.ShapeDtypeStruct((80, 80), jnp.float32),
         ),
         in_specs=[anywhere] * len(sources),
-        out_specs=(vmem, vmem),
+        out_specs=(anywhere, vmem),
         scratch_shapes=[pltpu.VMEM(source.shape, source.dtype) for source in sources]
-        + [pltpu.SemaphoreType.DMA((len(sources),))],
+        + [
+            pltpu.VMEM((devices, send_rows, LANES), jnp.bfloat16),
+            pltpu.SemaphoreType.DMA((len(sources),)),
+            pltpu.SemaphoreType.DMA((1 + devices,)),
+        ],
         compiler_params=pltpu.CompilerParams(vmem_limit_bytes=PREPARE_VMEM_LIMIT),
         name="prepare",
     )(*sources)

time: 91.5 us -> 89.1 us (0.974)
  waiting for transfers between devices: 46.3 us -> 44.6 us
    all_to_all x1, waiting for transfers between devices: 44.3 us -> 42.6 us  [one_stream_each(): got = lax.all_to_all(send, 'seq', split_axis=0, concat_axis=0, tiled=True)]
where the time goes in v3:
time: 89.1 us; the launch traced here: 88.9 us
  waiting for transfers between devices  44.6 us (50%)
  blocking collectives  21.2 us (24%)
  Pallas kernels  11.7 us (13%)
  starting transfers between devices  10.5 us (12%)
    all_to_all x1, waiting for transfers between devices, one_stream_each(): got = lax.all_to_all(send, 'seq', split_axis=0, concat_axis=0, tiled=True)  42.6 us
    all_to_all x1, blocking collectives, one_stream_each(): lax.all_to_all(payload, 'seq', split_axis=0, concat_axis=0, tiled=True)  21.2 us
    all_to_all x1, starting transfers between devices, one_stream_each(): got = lax.all_to_all(send, 'seq', split_axis=0, concat_axis=0, tiled=True)  7.4 us
    pallas_call x1, Pallas kernels, one_stream_each(): pl.pallas_call(functools.partial(prepare_kernel, devices=devices, columns...  4.74 us
    pallas_call x1, Pallas kernels, one_stream_each(): pl.pallas_call(functools.partial(attend_kernel, table_rows=table_rows), o...  3.5 us
    pallas_call x1, Pallas kernels, one_stream_each(): pl.pallas_call(functools.partial(finish_kernel, devices=devices, columns=...  2.08 us
    ppermute x1, waiting for transfers between devices, one_stream_each(): other_ids = lax.ppermute(adapter_ids, 'rep', swap)  2.05 us
  transfers between devices with their start and end apart: 3, of which 2 were waited for; matrix products, arithmetic and copies ran while one was open for 0% of the time, Pallas kernels for 4%

profile of v3, /device:TPU:0, one launch (start us, length us, event | category | flops | bytes accessed | tf_op | source)
XLA Modules:
  0.0 88.9 jit_solution(14546634574378361679)
XLA Ops:
  0.6 4.7 %prepare.1 = (bf16[16,584,128]{2,1,0:T(8,128)(2,1)}, f32[80,80]{1,0:T(8,128)}) custom-call(bf16[2,16,5120]{2,1,0:T(8,128)(2,1)} %refs_0_.1, bf16[2,16,5120]{2,1,0:T(8,128)(2,1)} %refs_1_.1, bf16[2,16,5120]{2,1,0:T(8,128)(2,1)} %refs_2_.1, bf16[2,16,5120]{2,1,0:T(8,128)(2,1)} %refs_3_.1, bf16[64,5120]{1,0:T(8,128)(2,1)} %refs_4_.1, f32[1,5120]{1,0:T(1,128)} %bitcast.15, ...), custom_call_target="tpu_custom_call" | custom-call | tf_op jit(solution)/shard_map/prepare/pallas_call | solution.py:551
  5.4 0.0 copy-start.5
  5.4 7.4 %all-to-all-start = ((bf16[16,584,128]{2,1,0:T(8,128)(2,1)}), bf16[16,584,128]{2,1,0:T(8,128)(2,1)S(1)}, u32[]{:S(2)}, u32[]{:S(2)}) async-start(bf16[16,584,128]{2,1,0:T(8,128)(2,1)} %get-tuple-element.7), calls=%async_computation | async-start | bytes 4784128 | tf_op jit(solution)/shard_map/all_to_all | solution.py:570
  12.8 0.0 copy-done.5
  12.8 0.0 copy-start
  12.8 0.0 copy-start.1
  12.8 0.0 copy-start.8
  12.8 0.0 copy-start.9
  12.9 0.0 copy-start.10
  12.9 1.6 %collective-permute-start = (s32[8]{0:T(128)S(1)}, s32[8]{0:T(128)S(1)}, u32[]{:S(2)}, u32[]{:S(2)}) collective-permute-start(s32[8]{0:T(128)S(1)} %copy-done.5), channel_id=1, source_target_pairs={{0,16},{16,0},{1,17},{17,1},{2,18},{18,2},{3,19},{19,3},{4,20},{20... | collective-permute-start | bytes 104 | tf_op jit(solution)/shard_map/ppermute | solution.py:535
  14.4 2.0 %collective-permute-done.ids_ref = s32[8]{0:T(128)S(1)} collective-permute-done((s32[8]{0:T(128)S(1)}, s32[8]{0:T(128)S(1)}, u32[]{:S(2)}, u32[]{:S(2)}) %collective-permute-start) | collective-permute-done | bytes 64 | tf_op jit(solution)/shard_map/ppermute | solution.py:535
  16.5 42.6 %all-to-all-done.got_ref.near_ref = bf16[16,584,128]{2,1,0:T(8,128)(2,1)S(1)} async-done(((bf16[16,584,128]{2,1,0:T(8,128)(2,1)}), bf16[16,584,128]{2,1,0:T(8,128)(2,1)S(1)}, u32[]{:S(2)}, u32[]{:S(2)}) %all-to-all-start) | async-done | bytes 2392096 | tf_op jit(solution)/shard_map/all_to_all | solution.py:570
  59.0 0.0 copy-start.2
  59.0 0.0 copy-start.3
  59.0 1.3 %choose.1 = bf16[8,264,128]{2,1,0:T(8,128)(2,1)S(1)} custom-call(s32[8]{0:T(128)S(1)} %collective-permute-done.ids_ref, bf16[16,584,128]{2,1,0:T(8,128)(2,1)S(1)} %all-to-all-done.got_ref.near_ref), custom_call_target="tpu_custom_call" | custom-call | tf_op jit(solution)/shard_map/choose/pallas_call | solution.py:572
  60.4 1.6 %collective-permute-start.1 = (bf16[8,264,128]{2,1,0:T(8,128)(2,1)S(1)}, bf16[8,264,128]{2,1,0:T(8,128)(2,1)S(1)}, u32[]{:S(2)}, u32[]{:S(2)}) collective-permute-start(bf16[8,264,128]{2,1,0:T(8,128)(2,1)S(1)} %choose.1), channel_id=1, source_target_pairs={{0,16},{16,0},{1,17},{17,1},{2,18},{18,2},{3,19},{19,3},{4,20},{20... | collective-permute-start | bytes 1622024 | tf_op jit(solution)/shard_map/ppermute | solution.py:581
  61.9 0.0 copy-done
  61.9 0.0 copy-done.1
  61.9 0.0 copy-done.2
  61.9 0.0 copy-done.3
  61.9 0.1 modulate.1
  62.0 0.0 copy-start.4
  62.0 0.0 copy-start.6
  62.0 0.0 copy-start.7
  62.1 0.0 copy-done.8
  62.1 0.0 copy-done.9
  62.1 0.0 copy-done.10
  62.1 3.5 %attend.1 = f32[16,24,128]{2,1,0:T(8,128)S(1)} custom-call(s32[8]{0:T(128)S(1)} %copy-done.9, bf16[16,584,128]{2,1,0:T(8,128)(2,1)S(1)} %all-to-all-done.got_ref.near_ref, f32[3,8,1280]{2,1,0:T(8,128)S(1)} %get-tuple-element.8.rows_ref, bf16[256,1280]{1,0:T(8,128)(2,1)S(1)} %get-tuple-element.9.head_ref, f32[1,64]{1,0:T(1,128)S(1)} %bitcast.12, ...), custom_call_target="tpu_custom_call" | custom-call | flops 1000000000 | bytes 4000000 | tf_op jit(solution)/shard_map/attend/pallas_call | solution.py:597
  65.6 21.2 %all_to_all.10 = f32[16,24,128]{2,1,0:T(8,128)S(1)} all-to-all(f32[16,24,128]{2,1,0:T(8,128)S(1)} %attend.1), channel_id=1, replica_groups=mesh['rep'=2,'seq'=16] {'seq'}, dimensions={0} | all-to-all | bytes 393216 | tf_op jit(solution)/shard_map/all_to_all | solution.py:619
  86.8 0.0 collective-permute-done.1.far_ref
  86.8 0.0 copy-done.4
  86.8 0.0 copy-done.6
  86.8 0.0 copy-done.7
  86.8 2.1 %finish.1 = (f32[2,8,64]{2,1,0:T(8,128)}, f32[2,8,64]{2,1,0:T(8,128)}, bf16[32,8,960]{2,1,0:T(8,128)(2,1)}) custom-call(s32[8]{0:T(128)S(1)} %copy-done.5, f32[384,128]{1,0:T(8,128)S(1)} %bitcast.10, f32[8]{0:T(128)S(1)} %copy-done.6, s32[8]{0:T(128)S(1)} %copy-done.7, f32[80,80]{1,0:T(8,128)S(1)} %copy-done.4, ...), custom_call_target="tpu_custom_call" | custom-call | tf_op jit(solution)/shard_map/finish/pallas_call | solution.py:622
Async XLA Ops:
  5.4 7.4 %copy-start.5 = (s32[8]{0:T(128)S(1)}, s32[8]{0:T(128)}, u32[]{:S(2)}) copy-start(s32[8]{0:T(128)} %ids_ref.1) | copy-start | bytes 100
  5.4 53.6 %all-to-all-start = ((bf16[16,584,128]{2,1,0:T(8,128)(2,1)}), bf16[16,584,128]{2,1,0:T(8,128)(2,1)S(1)}, u32[]{:S(2)}, u32[]{:S(2)}) async-start(bf16[16,584,128]{2,1,0:T(8,128)(2,1)} %get-tuple-element.7), calls=%async_computation | async-start | bytes 4784128 | tf_op jit(solution)/shard_map/all_to_all | solution.py:570
  12.8 49.1 %copy-start = (bf16[5120,64]{0,1:T(8,128)(2,1)S(1)}, bf16[5120,64]{0,1:T(8,128)(2,1)}, u32[]{:S(2)}) copy-start(bf16[5120,64]{0,1:T(8,128)(2,1)} %param.25) | copy-start | bytes 1966084
  12.8 49.1 %copy-start.1 = (f32[16,5120]{1,0:T(8,128)S(1)}, f32[16,5120]{1,0:T(8,128)}, u32[]{:S(2)}) copy-start(f32[16,5120]{1,0:T(8,128)} %gate_ref.1) | copy-start | bytes 983044
  12.8 49.2 %copy-start.8 = (f32[2,8,64]{2,1,0:T(8,128)S(1)}, f32[2,8,64]{2,1,0:T(8,128)}, u32[]{:S(2)}) copy-start(f32[2,8,64]{2,1,0:T(8,128)} %latent_ref.1) | copy-start | bytes 12292
  12.8 49.2 %copy-start.9 = (s32[8]{0:T(128)S(1)}, s32[8]{0:T(128)}, u32[]{:S(2)}) copy-start(s32[8]{0:T(128)} %lengths_ref.1) | copy-start | bytes 100
  12.9 49.2 %copy-start.10 = (f32[64]{0:T(128)S(1)}, f32[64]{0:T(128)}, u32[]{:S(2)}) copy-start(f32[64]{0:T(128)} %param.26) | copy-start | bytes 772
  12.9 3.6 %collective-permute-start = (s32[8]{0:T(128)S(1)}, s32[8]{0:T(128)S(1)}, u32[]{:S(2)}, u32[]{:S(2)}) collective-permute-start(s32[8]{0:T(128)S(1)} %copy-done.5), channel_id=1, source_target_pairs={{0,16},{16,0},{1,17},{17,1},{2,18},{18,2},{3,19},{19,3},{4,20},{20... | collective-permute-start | bytes 104 | tf_op jit(solution)/shard_map/ppermute | solution.py:535
  59.0 2.9 %copy-start.2 = (f32[16,5120]{1,0:T(8,128)S(1)}, f32[16,5120]{1,0:T(8,128)}, u32[]{:S(2)}) copy-start(f32[16,5120]{1,0:T(8,128)} %shift_ref.1) | copy-start | bytes 983044
  59.0 2.9 %copy-start.3 = (f32[16,5120]{1,0:T(8,128)S(1)}, f32[16,5120]{1,0:T(8,128)}, u32[]{:S(2)}) copy-start(f32[16,5120]{1,0:T(8,128)} %scale_ref.1) | copy-start | bytes 983044
  60.4 26.4 %collective-permute-start.1 = (bf16[8,264,128]{2,1,0:T(8,128)(2,1)S(1)}, bf16[8,264,128]{2,1,0:T(8,128)(2,1)S(1)}, u32[]{:S(2)}, u32[]{:S(2)}) collective-permute-start(bf16[8,264,128]{2,1,0:T(8,128)(2,1)S(1)} %choose.1), channel_id=1, source_target_pairs={{0,16},{16,0},{1,17},{17,1},{2,18},{18,2},{3,19},{19,3},{4,20},{20... | collective-permute-start | bytes 1622024 | tf_op jit(solution)/shard_map/ppermute | solution.py:581
  62.0 24.8 %copy-start.4 = (f32[80,80]{1,0:T(8,128)S(1)}, f32[80,80]{1,0:T(8,128)}, u32[]{:S(2)}) copy-start(f32[80,80]{1,0:T(8,128)} %get-tuple-element.10.gram_ref) | copy-start | bytes 76804
  62.0 24.8 %copy-start.6 = (f32[8]{0:T(128)S(1)}, f32[8]{0:T(128)}, u32[]{:S(2)}) copy-start(f32[8]{0:T(128)} %guidance_ref.1) | copy-start | bytes 100
  62.0 24.8 %copy-start.7 = (s32[8]{0:T(128)S(1)}, s32[8]{0:T(128)}, u32[]{:S(2)}) copy-start(s32[8]{0:T(128)} %step_ref.1) | copy-start | bytes 100

commit v4 on v3

--- a/solution.py
+++ b/solution.py
@@ -128,20 +128,10 @@
         write.wait()
 
 
-def choose_kernel(ids_ref, got_ref, out_ref, sems):
+def choose_kernel(ids_ref, got_ref, out_ref):
     count = out_ref.shape[1]
-    copies = [
-        pltpu.make_async_copy(
-            got_ref.at[ids_ref[request], 0:count],
-            out_ref.at[request],
-            sems.at[request],
-        )
-        for request in range(REQUESTS)
-    ]
-    for copy in copies:
-        copy.start()
-    for copy in copies:
-        copy.wait()
+    for request in range(REQUESTS):
+        out_ref[request] = got_ref[ids_ref[request], 0:count, :]
 
 
 def group_sum(x):
@@ -572,9 +562,8 @@
     chosen = pl.pallas_call(
         choose_kernel,
         out_shape=jax.ShapeDtypeStruct((REQUESTS, table_rows, LANES), jnp.bfloat16),
-        in_specs=[smem, anywhere],
-        out_specs=anywhere,
-        scratch_shapes=[pltpu.SemaphoreType.DMA((REQUESTS,))],
+        in_specs=[smem, vmem],
+        out_specs=vmem,
         compiler_params=params,
         name="choose",
     )(other_ids, got)

time: 89.1 us -> 88.4 us (level)
  no operation moved by 1% of the time
where the time goes in v4:
time: 88.4 us; the launch traced here: 88.2 us
  waiting for transfers between devices  44.6 us (50%)
  blocking collectives  21.2 us (24%)
  Pallas kernels  11 us (12%)
  starting transfers between devices  10.5 us (12%)
    all_to_all x1, waiting for transfers between devices, one_stream_each(): got = lax.all_to_all(send, 'seq', split_axis=0, concat_axis=0, tiled=True)  42.6 us
    all_to_all x1, blocking collectives, one_stream_each(): lax.all_to_all(payload, 'seq', split_axis=0, concat_axis=0, tiled=True)  21.2 us
    all_to_all x1, starting transfers between devices, one_stream_each(): got = lax.all_to_all(send, 'seq', split_axis=0, concat_axis=0, tiled=True)  7.4 us
    pallas_call x1, Pallas kernels, one_stream_each(): pl.pallas_call(functools.partial(prepare_kernel, devices=devices, columns...  4.74 us
    pallas_call x1, Pallas kernels, one_stream_each(): pl.pallas_call(functools.partial(attend_kernel, table_rows=table_rows), o...  3.51 us
    pallas_call x1, Pallas kernels, one_stream_each(): pl.pallas_call(functools.partial(finish_kernel, devices=devices, columns=...  2.08 us
    ppermute x1, waiting for transfers between devices, one_stream_each(): other_ids = lax.ppermute(adapter_ids, 'rep', swap)  2.05 us
  transfers between devices with their start and end apart: 3, of which 2 were waited for; matrix products, arithmetic and copies ran while one was open for 0% of the time, Pallas kernels for 4%

profile of v4, /device:TPU:0, one launch (start us, length us, event | category | flops | bytes accessed | tf_op | source)
XLA Modules:
  0.0 88.2 jit_solution(4436686312149189954)
XLA Ops:
  0.6 4.7 %prepare.1 = (bf16[16,584,128]{2,1,0:T(8,128)(2,1)}, f32[80,80]{1,0:T(8,128)}) custom-call(bf16[2,16,5120]{2,1,0:T(8,128)(2,1)} %refs_0_.1, bf16[2,16,5120]{2,1,0:T(8,128)(2,1)} %refs_1_.1, bf16[2,16,5120]{2,1,0:T(8,128)(2,1)} %refs_2_.1, bf16[2,16,5120]{2,1,0:T(8,128)(2,1)} %refs_3_.1, bf16[64,5120]{1,0:T(8,128)(2,1)} %refs_4_.1, f32[1,5120]{1,0:T(1,128)} %bitcast.15, ...), custom_call_target="tpu_custom_call" | custom-call | tf_op jit(solution)/shard_map/prepare/pallas_call | solution.py:541
  5.4 0.0 copy-start.5
  5.4 7.4 %all-to-all-start = ((bf16[16,584,128]{2,1,0:T(8,128)(2,1)}), bf16[16,584,128]{2,1,0:T(8,128)(2,1)S(1)}, u32[]{:S(2)}, u32[]{:S(2)}) async-start(bf16[16,584,128]{2,1,0:T(8,128)(2,1)} %get-tuple-element.7), calls=%async_computation | async-start | bytes 4784128 | tf_op jit(solution)/shard_map/all_to_all | solution.py:560
  12.8 0.0 copy-done.5
  12.8 0.0 copy-start
  12.8 0.0 copy-start.1
  12.8 0.0 copy-start.8
  12.8 0.0 copy-start.9
  12.9 0.0 copy-start.10
  12.9 1.6 %collective-permute-start = (s32[8]{0:T(128)S(1)}, s32[8]{0:T(128)S(1)}, u32[]{:S(2)}, u32[]{:S(2)}) collective-permute-start(s32[8]{0:T(128)S(1)} %copy-done.5), channel_id=1, source_target_pairs={{0,16},{16,0},{1,17},{17,1},{2,18},{18,2},{3,19},{19,3},{4,20},{20... | collective-permute-start | bytes 104 | tf_op jit(solution)/shard_map/ppermute | solution.py:525
  14.4 2.0 %collective-permute-done.ids_ref = s32[8]{0:T(128)S(1)} collective-permute-done((s32[8]{0:T(128)S(1)}, s32[8]{0:T(128)S(1)}, u32[]{:S(2)}, u32[]{:S(2)}) %collective-permute-start) | collective-permute-done | bytes 64 | tf_op jit(solution)/shard_map/ppermute | solution.py:525
  16.5 42.6 %all-to-all-done.got_ref.near_ref = bf16[16,584,128]{2,1,0:T(8,128)(2,1)S(1)} async-done(((bf16[16,584,128]{2,1,0:T(8,128)(2,1)}), bf16[16,584,128]{2,1,0:T(8,128)(2,1)S(1)}, u32[]{:S(2)}, u32[]{:S(2)}) %all-to-all-start) | async-done | bytes 2392096 | tf_op jit(solution)/shard_map/all_to_all | solution.py:560
  59.0 0.0 copy-start.2
  59.0 0.0 copy-start.3
  59.0 0.6 choose.1
  59.6 1.6 %collective-permute-start.1 = (bf16[8,264,128]{2,1,0:T(8,128)(2,1)S(1)}, bf16[8,264,128]{2,1,0:T(8,128)(2,1)S(1)}, u32[]{:S(2)}, u32[]{:S(2)}) collective-permute-start(bf16[8,264,128]{2,1,0:T(8,128)(2,1)S(1)} %choose.1), channel_id=1, source_target_pairs={{0,16},{16,0},{1,17},{17,1},{2,18},{18,2},{3,19},{19,3},{4,20},{20... | collective-permute-start | bytes 1622024 | tf_op jit(solution)/shard_map/ppermute | solution.py:570
  61.2 0.0 copy-done
  61.2 0.0 copy-done.1
  61.2 0.0 copy-done.2
  61.2 0.0 copy-done.3
  61.2 0.1 modulate.1
  61.3 0.0 copy-start.4
  61.3 0.0 copy-start.6
  61.3 0.0 copy-start.7
  61.3 0.0 copy-done.8
  61.3 0.0 copy-done.9
  61.4 0.0 copy-done.10
  61.4 3.5 %attend.1 = f32[16,24,128]{2,1,0:T(8,128)S(1)} custom-call(s32[8]{0:T(128)S(1)} %copy-done.9, bf16[16,584,128]{2,1,0:T(8,128)(2,1)S(1)} %all-to-all-done.got_ref.near_ref, f32[3,8,1280]{2,1,0:T(8,128)S(1)} %get-tuple-element.8.rows_ref, bf16[256,1280]{1,0:T(8,128)(2,1)S(1)} %get-tuple-element.9.head_ref, f32[1,64]{1,0:T(1,128)S(1)} %bitcast.12, ...), custom_call_target="tpu_custom_call" | custom-call | flops 1000000000 | bytes 4000000 | tf_op jit(solution)/shard_map/attend/pallas_call | solution.py:586
  64.9 21.2 %all_to_all.10 = f32[16,24,128]{2,1,0:T(8,128)S(1)} all-to-all(f32[16,24,128]{2,1,0:T(8,128)S(1)} %attend.1), channel_id=1, replica_groups=mesh['rep'=2,'seq'=16] {'seq'}, dimensions={0} | all-to-all | bytes 393216 | tf_op jit(solution)/shard_map/all_to_all | solution.py:608
  86.1 0.0 collective-permute-done.1.far_ref
  86.1 0.0 copy-done.4
  86.1 0.0 copy-done.6
  86.1 0.0 copy-done.7
  86.1 2.1 %finish.1 = (f32[2,8,64]{2,1,0:T(8,128)}, f32[2,8,64]{2,1,0:T(8,128)}, bf16[32,8,960]{2,1,0:T(8,128)(2,1)}) custom-call(s32[8]{0:T(128)S(1)} %copy-done.5, f32[384,128]{1,0:T(8,128)S(1)} %bitcast.10, f32[8]{0:T(128)S(1)} %copy-done.6, s32[8]{0:T(128)S(1)} %copy-done.7, f32[80,80]{1,0:T(8,128)S(1)} %copy-done.4, ...), custom_call_target="tpu_custom_call" | custom-call | tf_op jit(solution)/shard_map/finish/pallas_call | solution.py:611
Async XLA Ops:
  5.4 7.4 %copy-start.5 = (s32[8]{0:T(128)S(1)}, s32[8]{0:T(128)}, u32[]{:S(2)}) copy-start(s32[8]{0:T(128)} %ids_ref.1) | copy-start | bytes 100
  5.4 53.6 %all-to-all-start = ((bf16[16,584,128]{2,1,0:T(8,128)(2,1)}), bf16[16,584,128]{2,1,0:T(8,128)(2,1)S(1)}, u32[]{:S(2)}, u32[]{:S(2)}) async-start(bf16[16,584,128]{2,1,0:T(8,128)(2,1)} %get-tuple-element.7), calls=%async_computation | async-start | bytes 4784128 | tf_op jit(solution)/shard_map/all_to_all | solution.py:560
  12.8 48.4 %copy-start = (bf16[5120,64]{0,1:T(8,128)(2,1)S(1)}, bf16[5120,64]{0,1:T(8,128)(2,1)}, u32[]{:S(2)}) copy-start(bf16[5120,64]{0,1:T(8,128)(2,1)} %param.25) | copy-start | bytes 1966084
  12.8 48.4 %copy-start.1 = (f32[16,5120]{1,0:T(8,128)S(1)}, f32[16,5120]{1,0:T(8,128)}, u32[]{:S(2)}) copy-start(f32[16,5120]{1,0:T(8,128)} %gate_ref.1) | copy-start | bytes 983044
  12.8 48.5 %copy-start.8 = (f32[2,8,64]{2,1,0:T(8,128)S(1)}, f32[2,8,64]{2,1,0:T(8,128)}, u32[]{:S(2)}) copy-start(f32[2,8,64]{2,1,0:T(8,128)} %latent_ref.1) | copy-start | bytes 12292
  12.8 48.5 %copy-start.9 = (s32[8]{0:T(128)S(1)}, s32[8]{0:T(128)}, u32[]{:S(2)}) copy-start(s32[8]{0:T(128)} %lengths_ref.1) | copy-start | bytes 100
  12.9 48.5 %copy-start.10 = (f32[64]{0:T(128)S(1)}, f32[64]{0:T(128)}, u32[]{:S(2)}) copy-start(f32[64]{0:T(128)} %param.26) | copy-start | bytes 772
  12.9 3.6 %collective-permute-start = (s32[8]{0:T(128)S(1)}, s32[8]{0:T(128)S(1)}, u32[]{:S(2)}, u32[]{:S(2)}) collective-permute-start(s32[8]{0:T(128)S(1)} %copy-done.5), channel_id=1, source_target_pairs={{0,16},{16,0},{1,17},{17,1},{2,18},{18,2},{3,19},{19,3},{4,20},{20... | collective-permute-start | bytes 104 | tf_op jit(solution)/shard_map/ppermute | solution.py:525
  59.0 2.2 %copy-start.2 = (f32[16,5120]{1,0:T(8,128)S(1)}, f32[16,5120]{1,0:T(8,128)}, u32[]{:S(2)}) copy-start(f32[16,5120]{1,0:T(8,128)} %shift_ref.1) | copy-start | bytes 983044
  59.0 2.2 %copy-start.3 = (f32[16,5120]{1,0:T(8,128)S(1)}, f32[16,5120]{1,0:T(8,128)}, u32[]{:S(2)}) copy-start(f32[16,5120]{1,0:T(8,128)} %scale_ref.1) | copy-start | bytes 983044
  59.6 26.4 %collective-permute-start.1 = (bf16[8,264,128]{2,1,0:T(8,128)(2,1)S(1)}, bf16[8,264,128]{2,1,0:T(8,128)(2,1)S(1)}, u32[]{:S(2)}, u32[]{:S(2)}) collective-permute-start(bf16[8,264,128]{2,1,0:T(8,128)(2,1)S(1)} %choose.1), channel_id=1, source_target_pairs={{0,16},{16,0},{1,17},{17,1},{2,18},{18,2},{3,19},{19,3},{4,20},{20... | collective-permute-start | bytes 1622024 | tf_op jit(solution)/shard_map/ppermute | solution.py:570
  61.3 24.8 %copy-start.4 = (f32[80,80]{1,0:T(8,128)S(1)}, f32[80,80]{1,0:T(8,128)}, u32[]{:S(2)}) copy-start(f32[80,80]{1,0:T(8,128)} %get-tuple-element.10.gram_ref) | copy-start | bytes 76804
  61.3 24.8 %copy-start.6 = (f32[8]{0:T(128)S(1)}, f32[8]{0:T(128)}, u32[]{:S(2)}) copy-start(f32[8]{0:T(128)} %guidance_ref.1) | copy-start | bytes 100
  61.3 24.8 %copy-start.7 = (s32[8]{0:T(128)S(1)}, s32[8]{0:T(128)}, u32[]{:S(2)}) copy-start(s32[8]{0:T(128)} %step_ref.1) | copy-start | bytes 100

commit v5 on v4

--- a/solution.py
+++ b/solution.py
@@ -15,6 +15,7 @@
 QUARTERS = 4
 TABLE_ROWS = 64
 BIAS_ROWS = 8
+LATENT_ROW = 4
 VMEM_LIMIT = 20 << 20
 PREPARE_VMEM_LIMIT = 56 << 20
 
@@ -26,15 +27,15 @@
 
 
 def prepare_kernel(*refs, devices, columns, half_tiles):
-    sources, (sent_ref, gram_ref), held = refs[:8], refs[8:10], refs[10:18]
-    send_ref, sems, out_sems = refs[18:]
+    sources, (sent_ref, gram_ref), held = refs[:9], refs[9:11], refs[11:20]
+    send_ref, sems, out_sems = refs[20:]
     copies = [
         pltpu.make_async_copy(source, target, sems.at[index])
         for index, (source, target) in enumerate(zip(sources, held))
     ]
     for copy in copies:
         copy.start()
-    q_ref, k_ref, v_ref, h_ref, embed_ref, bias_ref, down_ref, up_ref = held
+    q_ref, k_ref, v_ref, h_ref, embed_ref, bias_ref, down_ref, latent_ref, up_ref = held
     row_count, stream_count, width = q_ref.shape
     quarter = width // QUARTERS
     tiles = quarter // LANES
@@ -69,7 +70,7 @@
     ]
     writes[0].start()
 
-    for copy in copies[4:7]:
+    for copy in copies[4:8]:
         copy.wait()
     bias = bias_ref[...]
     high = bias.astype(jnp.bfloat16).astype(jnp.float32)
@@ -84,7 +85,13 @@
     ones_at = 67
     sums = gram[:, ones_at : ones_at + 1]
     centered = raw - sums * (1.0 / width) * raw[ones_at : ones_at + 1, :]
-    gram_ref[...] = gram - sums * (1.0 / width) * gram[ones_at : ones_at + 1, :]
+    gram = gram - sums * (1.0 / width) * gram[ones_at : ones_at + 1, :]
+    gram = jnp.concatenate([gram, jnp.zeros((80, LANES - 80), jnp.float32)], axis=1)
+    gram_high = gram.astype(jnp.bfloat16)
+    left_over = gram - gram_high.astype(jnp.float32)
+    gram_middle = left_over.astype(jnp.bfloat16)
+    gram_low = (left_over - gram_middle.astype(jnp.float32)).astype(jnp.bfloat16)
+    gram_ref[...] = jnp.concatenate([gram_high, gram_middle, gram_low], axis=1)
     bias_row = centered[64:65] + centered[65:66] + centered[66:67]
     tail = lax.broadcasted_iota(jnp.int32, (8, centered.shape[1]), 0)
     mixing = jnp.concatenate(
@@ -96,7 +103,11 @@
 
     half = half_tiles * LANES
     side = lax.axis_index("rep") * half
-    copies[7].wait()
+    copies[8].wait()
+    latent = jnp.concatenate([latent_ref[0], latent_ref[1]], axis=1)
+    latent_high = latent.astype(jnp.bfloat16).astype(jnp.float32)
+    latent_middle = (latent - latent_high).astype(jnp.bfloat16).astype(jnp.float32)
+    latent_pieces = (latent_high, latent_middle, latent - latent_high - latent_middle)
     row = lax.broadcasted_iota(jnp.int32, (BIAS_ROWS, LANES), 0)
     for target in range(devices):
         start = columns * target // LANES * LANES
@@ -113,6 +124,13 @@
             biases = jnp.where(
                 row == tile,
                 jnp.broadcast_to(piece[TABLE_ROWS : TABLE_ROWS + 1], biases.shape),
+                biases,
+            )
+        request = target % REQUESTS
+        for index, piece in enumerate(latent_pieces):
+            biases = jnp.where(
+                row == LATENT_ROW + index,
+                jnp.broadcast_to(piece[request : request + 1], biases.shape),
                 biases,
             )
         send_ref[target, half_tiles * TABLE_ROWS : table_rows, :] = biases.astype(jnp.bfloat16)
@@ -161,13 +179,19 @@
         ]
 
 
+def sigma_change(position):
+    now = noise_level(position.astype(jnp.float32))
+    return noise_level((position + 1).astype(jnp.float32)) - now
+
+
 def attend_kernel(
     lengths_ref,
+    guidance_ref,
+    step_ref,
     got_ref,
     rows_ref,
     head_ref,
     bias_ref,
-    latent_ref,
     out_ref,
     residual_ref,
     pick_ref,
@@ -179,7 +203,8 @@
     width = quarter * QUARTERS
     tiles = quarter // LANES
     size = devices * 8
-    limit = lengths_ref[lax.axis_index("seq") % REQUESTS]
+    mine = lax.axis_index("seq")
+    limit = lengths_ref[mine % REQUESTS]
     score_scale = 1.0 / HEAD_DIM**0.5
 
     row = lax.broadcasted_iota(jnp.int32, (size, size), 0)
@@ -238,23 +263,27 @@
     second_token = pick_ref[pl.ds(1, devices, stride=8), :]
     lane = lax.broadcasted_iota(jnp.int32, (devices, LANES), 1)
     stream_velocity = jnp.where(lane < channels, first_token, second_token)
-    latent = jnp.concatenate([latent_ref[0], latent_ref[1]], axis=1)
-    block = jnp.concatenate([stream_velocity, latent], axis=0)
+    pieces = got_ref[:, table_rows - BIAS_ROWS : table_rows, :].astype(jnp.float32)
+    latent = sum(pieces[:, LATENT_ROW + index, :] for index in range(3))
+    guidance = jnp.full((devices, LANES), guidance_ref[mine % REQUESTS], jnp.float32)
+    change = sigma_change(jnp.full((devices, LANES), step_ref[mine % REQUESTS], jnp.int32))
+    conditional = latent + change * guidance * stream_velocity
+    unconditional = change * (1.0 - guidance) * stream_velocity
+    block = jnp.where(jnp.full((devices, LANES), mine, jnp.int32) < REQUESTS, conditional, unconditional)
     out_ref[...] = jnp.broadcast_to(block[None], out_ref.shape)
 
 
 def finish_kernel(
     ids_ref,
     got_ref,
-    guidance_ref,
     step_ref,
+    own_ref,
     gram_ref,
     near_ref,
     far_ref,
     velocity_ref,
     latent_ref,
     delta_ref,
-    velocity_all,
     latent_all,
     product_ref,
     *,
@@ -262,32 +291,27 @@
     columns,
     half_tiles,
 ):
-    block = devices + REQUESTS
+    block = devices
     request_row = lax.broadcasted_iota(jnp.int32, (REQUESTS, LANES), 0)
-    guidance = jnp.zeros((REQUESTS, LANES), jnp.float32)
     position = jnp.zeros((REQUESTS, LANES), jnp.int32)
     for request in range(REQUESTS):
-        guidance = jnp.where(request_row == request, guidance_ref[request], guidance)
         position = jnp.where(request_row == request, step_ref[request], position)
-    sigma_now = noise_level(position.astype(jnp.float32))
-    step = noise_level((position + 1).astype(jnp.float32)) - sigma_now
+    change = sigma_change(position)
     lane = lax.broadcasted_iota(jnp.int32, (REQUESTS, LANES), 1)
     channels = LANES // 2
     pieces = []
     for source in range(devices):
         conditional = got_ref[pl.ds(source, REQUESTS, stride=block), :]
         unconditional = got_ref[pl.ds(REQUESTS * block + source, REQUESTS, stride=block), :]
-        velocity = unconditional + guidance * (conditional - unconditional)
-        first = source * block + devices
-        latent_next = got_ref[first : first + REQUESTS, :] + step * velocity
-        velocity_all[source] = velocity
+        latent_next = conditional + unconditional
         latent_all[source] = latent_next
         tail = jnp.where(lane < channels + 3, 1.0, 0.0)
         pieces.append(jnp.where(lane < channels, latent_next, tail))
         pieces.append(jnp.where(lane < channels, pltpu.roll(latent_next, channels, 1), tail))
     mine = lax.axis_index("seq")
-    velocity = velocity_all[mine]
     latent_next = latent_all[mine]
+    own = jnp.concatenate([own_ref[0], own_ref[1]], axis=1)
+    velocity = (latent_next - own) / change
     velocity_ref[0] = velocity[:, :channels]
     velocity_ref[1] = velocity[:, channels:]
     latent_ref[0] = latent_next[:, :channels]
@@ -297,23 +321,22 @@
     rows = rounded.shape[0]
     exact = rounded.astype(jnp.float32)
     used = gram_ref.shape[0]
-    image = jnp.dot(
-        exact[:, :used],
-        gram_ref[...],
-        precision=lax.Precision.HIGHEST,
-        preferred_element_type=jnp.float32,
-    )
-    spread = jnp.sum(image * exact[:, :used], axis=-1, keepdims=True)
+    pieces = jnp.dot(rounded[:, :used], gram_ref[...], preferred_element_type=jnp.float32)
+    image = pieces[:, :LANES] + pieces[:, LANES : 2 * LANES] + pieces[:, 2 * LANES :]
+    spread = jnp.sum(image * exact, axis=-1, keepdims=True)
     inverse = lax.rsqrt(spread * (1.0 / (HEADS * HEAD_DIM)) + 1e-06)
 
-    request_of_row = lax.broadcasted_iota(jnp.int32, (rows, TABLE_ROWS), 0) % REQUESTS
+    row = lax.broadcasted_iota(jnp.int32, (rows, LANES), 0) % REQUESTS
+    column = lax.broadcasted_iota(jnp.int32, (rows, LANES), 1)
+    twice = jnp.where(column < channels, exact, pltpu.roll(exact, channels, 1))
+    request_here = row - jnp.where(column < channels, 0, 1)
     left = jnp.concatenate(
         [
-            jnp.where(request_of_row == request, exact[:, :TABLE_ROWS], 0.0)
-            for request in range(REQUESTS)
+            jnp.where(request_here == request, twice, 0.0).astype(jnp.bfloat16)
+            for request in range(0, REQUESTS, 2)
         ],
         axis=1,
-    ).astype(jnp.bfloat16)
+    )
     half = half_tiles * LANES
     side = lax.axis_index("rep")
 
@@ -536,6 +559,7 @@
         embed_weight,
         embed_bias[None, :],
         adapter_down[0].T,
+        latent,
         adapter_up[0].T,
     )
     send, gram = pl.pallas_call(
@@ -544,7 +568,7 @@
         ),
         out_shape=(
             jax.ShapeDtypeStruct((devices, send_rows, LANES), jnp.bfloat16),
-            jax.ShapeDtypeStruct((80, 80), jnp.float32),
+            jax.ShapeDtypeStruct((80, 3 * LANES), jnp.bfloat16),
         ),
         in_specs=[anywhere] * len(sources),
         out_specs=(anywhere, vmem),
@@ -582,11 +606,11 @@
         compiler_params=params,
         name="modulate",
     )(residual_gate, head_shift, head_scale, head_weight.T)
-    payload_rows = devices + REQUESTS
+    payload_rows = devices
     payload = pl.pallas_call(
         functools.partial(attend_kernel, table_rows=table_rows),
         out_shape=jax.ShapeDtypeStruct((devices, payload_rows, LANES), jnp.float32),
-        in_specs=[smem] + [vmem] * 5,
+        in_specs=[smem] * 3 + [vmem] * 4,
         out_specs=vmem,
         scratch_shapes=[
             pltpu.VMEM((quarter // LANES, devices * 8, LANES), jnp.float32),
@@ -599,11 +623,12 @@
         ),
     )(
         lengths,
+        guidance,
+        step_index,
         got,
         rows,
         head,
         head_bias[None, :],
-        latent,
     )
     shared = lax.all_to_all(payload, "seq", split_axis=0, concat_axis=0, tiled=True)
 
@@ -615,10 +640,9 @@
             jax.ShapeDtypeStruct(latent.shape, jnp.float32),
             jax.ShapeDtypeStruct((row_count * devices, REQUESTS, columns), jnp.bfloat16),
         ),
-        in_specs=[smem, vmem, smem, smem] + [vmem] * 3,
+        in_specs=[smem, vmem, smem] + [vmem] * 4,
         out_specs=(vmem, vmem, vmem),
         scratch_shapes=[
-            pltpu.VMEM((devices,) + across, jnp.float32),
             pltpu.VMEM((devices,) + across, jnp.float32),
             pltpu.VMEM((row_count * devices * REQUESTS, 2 * half_tiles * LANES), jnp.float32),
         ],
@@ -627,8 +651,8 @@
     )(
         adapter_ids,
         shared.reshape(devices * payload_rows, LANES),
-        guidance,
         step_index,
+        latent,
         gram,
         got,
         far,
@@ -653,6 +677,7 @@
         and held.shape[0] == 1
         and held.shape[2] == LANES // 2
         and lax.axis_size("rep") == 2
+        and window_tiles(columns, devices) // 2 <= LATENT_ROW
         and width % (QUARTERS * LANES) == 0
         and all(
             columns * d // LANES + window_tiles(columns, devices) <= table.shape[1] // LANES

time: 88.4 us -> 87.2 us (0.986)
  blocking collectives: 21.2 us -> 20.1 us
    all_to_all x1, blocking collectives: 21.2 us -> 20.1 us  [one_stream_each(): lax.all_to_all(payload, 'seq', split_axis=0, concat_axis=0, tiled=True)]
where the time goes in v5:
time: 87.2 us; the launch traced here: 87 us
  waiting for transfers between devices  44.6 us (51%)
  blocking collectives  20.1 us (23%)
  Pallas kernels  10.9 us (12%)
  starting transfers between devices  10.5 us (12%)
    all_to_all x1, waiting for transfers between devices, one_stream_each(): got = lax.all_to_all(send, 'seq', split_axis=0, concat_axis=0, tiled=True)  42.6 us
    all_to_all x1, blocking collectives, one_stream_each(): lax.all_to_all(payload, 'seq', split_axis=0, concat_axis=0, tiled=True)  20.1 us
    all_to_all x1, starting transfers between devices, one_stream_each(): got = lax.all_to_all(send, 'seq', split_axis=0, concat_axis=0, tiled=True)  7.4 us
    pallas_call x1, Pallas kernels, one_stream_each(): pl.pallas_call(functools.partial(prepare_kernel, devices=devices, columns...  4.76 us
    pallas_call x1, Pallas kernels, one_stream_each(): pl.pallas_call(functools.partial(attend_kernel, table_rows=table_rows), o...  3.52 us
    ppermute x1, waiting for transfers between devices, one_stream_each(): other_ids = lax.ppermute(adapter_ids, 'rep', swap)  2.05 us
    pallas_call x1, Pallas kernels, one_stream_each(): pl.pallas_call(functools.partial(finish_kernel, devices=devices, columns=...  1.96 us
  transfers between devices with their start and end apart: 3, of which 2 were waited for; matrix products, arithmetic and copies ran while one was open for 0% of the time, Pallas kernels for 4%

profile of v5, /device:TPU:0, one launch (start us, length us, event | category | flops | bytes accessed | tf_op | source)
XLA Modules:
  0.0 87.0 jit_solution(14715899781868892596)
XLA Ops:
  0.6 4.8 %prepare.1 = (bf16[16,584,128]{2,1,0:T(8,128)(2,1)}, bf16[80,384]{1,0:T(8,128)(2,1)}) custom-call(bf16[2,16,5120]{2,1,0:T(8,128)(2,1)} %refs_0_.1, bf16[2,16,5120]{2,1,0:T(8,128)(2,1)} %refs_1_.1, bf16[2,16,5120]{2,1,0:T(8,128)(2,1)} %refs_2_.1, bf16[2,16,5120]{2,1,0:T(8,128)(2,1)} %refs_3_.1, bf16[64,5120]{1,0:T(8,128)(2,1)} %refs_4_.1, ...), custom_call_target="tpu_custom_call" | custom-call | tf_op jit(solution)/shard_map/prepare/pallas_call | solution.py:565
  5.4 0.0 copy-start.6
  5.4 7.4 %all-to-all-start = ((bf16[16,584,128]{2,1,0:T(8,128)(2,1)}), bf16[16,584,128]{2,1,0:T(8,128)(2,1)S(1)}, u32[]{:S(2)}, u32[]{:S(2)}) async-start(bf16[16,584,128]{2,1,0:T(8,128)(2,1)} %get-tuple-element.7), calls=%async_computation | async-start | bytes 4784128 | tf_op jit(solution)/shard_map/all_to_all | solution.py:584
  12.8 0.0 copy-done.6
  12.8 0.0 copy-start
  12.8 0.0 copy-start.1
  12.9 0.0 copy-start.7
  12.9 0.0 copy-start.8
  12.9 0.0 copy-start.9
  12.9 0.0 copy-start.10
  12.9 1.6 %collective-permute-start = (s32[8]{0:T(128)S(1)}, s32[8]{0:T(128)S(1)}, u32[]{:S(2)}, u32[]{:S(2)}) collective-permute-start(s32[8]{0:T(128)S(1)} %copy-done.6), channel_id=1, source_target_pairs={{0,16},{16,0},{1,17},{17,1},{2,18},{18,2},{3,19},{19,3},{4,20},{20... | collective-permute-start | bytes 104 | tf_op jit(solution)/shard_map/ppermute | solution.py:548
  14.5 2.0 %collective-permute-done.ids_ref = s32[8]{0:T(128)S(1)} collective-permute-done((s32[8]{0:T(128)S(1)}, s32[8]{0:T(128)S(1)}, u32[]{:S(2)}, u32[]{:S(2)}) %collective-permute-start) | collective-permute-done | bytes 64 | tf_op jit(solution)/shard_map/ppermute | solution.py:548
  16.5 42.6 %all-to-all-done.got_ref.near_ref = bf16[16,584,128]{2,1,0:T(8,128)(2,1)S(1)} async-done(((bf16[16,584,128]{2,1,0:T(8,128)(2,1)}), bf16[16,584,128]{2,1,0:T(8,128)(2,1)S(1)}, u32[]{:S(2)}, u32[]{:S(2)}) %all-to-all-start) | async-done | bytes 2392096 | tf_op jit(solution)/shard_map/all_to_all | solution.py:584
  59.1 0.0 copy-start.2
  59.1 0.0 copy-start.3
  59.1 0.6 choose.1
  59.7 1.6 %collective-permute-start.1 = (bf16[8,264,128]{2,1,0:T(8,128)(2,1)S(1)}, bf16[8,264,128]{2,1,0:T(8,128)(2,1)S(1)}, u32[]{:S(2)}, u32[]{:S(2)}) collective-permute-start(bf16[8,264,128]{2,1,0:T(8,128)(2,1)S(1)} %choose.1), channel_id=1, source_target_pairs={{0,16},{16,0},{1,17},{17,1},{2,18},{18,2},{3,19},{19,3},{4,20},{20... | collective-permute-start | bytes 1622024 | tf_op jit(solution)/shard_map/ppermute | solution.py:594
  61.2 0.0 copy-done
  61.2 0.0 copy-done.1
  61.2 0.0 copy-done.2
  61.2 0.0 copy-done.3
  61.2 0.1 modulate.1
  61.3 0.0 copy-start.4
  61.3 0.0 copy-start.5
  61.3 0.0 copy-done.7
  61.4 0.0 copy-done.8
  61.4 0.0 copy-done.9
  61.4 0.0 copy-done.10
  61.4 3.5 %attend.1 = f32[16,16,128]{2,1,0:T(8,128)S(1)} custom-call(s32[8]{0:T(128)S(1)} %copy-done.8, f32[8]{0:T(128)S(1)} %copy-done.9, s32[8]{0:T(128)S(1)} %copy-done.7, bf16[16,584,128]{2,1,0:T(8,128)(2,1)S(1)} %all-to-all-done.got_ref.near_ref, f32[3,8,1280]{2,1,0:T(8,128)S(1)} %get-tuple-element.8.rows_ref, bf16[256,1280]{1,0:T(8,128)(2,1)S(1)} %get-tuple-element.9.head_ref, ...), custom_call_target="tpu_custom_call" | custom-call | flops 1000000000 | bytes 4000000 | tf_op jit(solution)/shard_map/attend/pallas_call | solution.py:610
  64.9 20.1 %all_to_all.10 = f32[16,16,128]{2,1,0:T(8,128)S(1)} all-to-all(f32[16,16,128]{2,1,0:T(8,128)S(1)} %attend.1), channel_id=1, replica_groups=mesh['rep'=2,'seq'=16] {'seq'}, dimensions={0} | all-to-all | bytes 262144 | tf_op jit(solution)/shard_map/all_to_all | solution.py:633
  85.0 0.0 collective-permute-done.1.far_ref
  85.0 0.0 copy-done.4
  85.1 0.0 copy-done.5
  85.1 2.0 %finish.1 = (f32[2,8,64]{2,1,0:T(8,128)}, f32[2,8,64]{2,1,0:T(8,128)}, bf16[32,8,960]{2,1,0:T(8,128)(2,1)}) custom-call(s32[8]{0:T(128)S(1)} %copy-done.6, f32[256,128]{1,0:T(8,128)S(1)} %bitcast.11, s32[8]{0:T(128)S(1)} %copy-done.7, f32[2,8,64]{2,1,0:T(8,128)S(1)} %copy-done.5, bf16[80,384]{1,0:T(8,128)(2,1)S(1)} %copy-done.4, ...), custom_call_target="tpu_custom_call" | custom-call | tf_op jit(solution)/shard_map/finish/pallas_call | solution.py:636
Async XLA Ops:
  5.4 7.4 %copy-start.6 = (s32[8]{0:T(128)S(1)}, s32[8]{0:T(128)}, u32[]{:S(2)}) copy-start(s32[8]{0:T(128)} %ids_ref.1) | copy-start | bytes 100
  5.4 53.6 %all-to-all-start = ((bf16[16,584,128]{2,1,0:T(8,128)(2,1)}), bf16[16,584,128]{2,1,0:T(8,128)(2,1)S(1)}, u32[]{:S(2)}, u32[]{:S(2)}) async-start(bf16[16,584,128]{2,1,0:T(8,128)(2,1)} %get-tuple-element.7), calls=%async_computation | async-start | bytes 4784128 | tf_op jit(solution)/shard_map/all_to_all | solution.py:584
  12.8 48.4 %copy-start = (bf16[5120,64]{0,1:T(8,128)(2,1)S(1)}, bf16[5120,64]{0,1:T(8,128)(2,1)}, u32[]{:S(2)}) copy-start(bf16[5120,64]{0,1:T(8,128)(2,1)} %param.25) | copy-start | bytes 1966084
  12.8 48.4 %copy-start.1 = (f32[16,5120]{1,0:T(8,128)S(1)}, f32[16,5120]{1,0:T(8,128)}, u32[]{:S(2)}) copy-start(f32[16,5120]{1,0:T(8,128)} %gate_ref.1) | copy-start | bytes 983044
  12.9 48.5 %copy-start.7 = (s32[8]{0:T(128)S(1)}, s32[8]{0:T(128)}, u32[]{:S(2)}) copy-start(s32[8]{0:T(128)} %step_ref.3) | copy-start | bytes 100
  12.9 48.5 %copy-start.8 = (s32[8]{0:T(128)S(1)}, s32[8]{0:T(128)}, u32[]{:S(2)}) copy-start(s32[8]{0:T(128)} %lengths_ref.1) | copy-start | bytes 100
  12.9 48.5 %copy-start.9 = (f32[8]{0:T(128)S(1)}, f32[8]{0:T(128)}, u32[]{:S(2)}) copy-start(f32[8]{0:T(128)} %guidance_ref.1) | copy-start | bytes 100
  12.9 48.5 %copy-start.10 = (f32[64]{0:T(128)S(1)}, f32[64]{0:T(128)}, u32[]{:S(2)}) copy-start(f32[64]{0:T(128)} %param.26) | copy-start | bytes 772
  12.9 3.6 %collective-permute-start = (s32[8]{0:T(128)S(1)}, s32[8]{0:T(128)S(1)}, u32[]{:S(2)}, u32[]{:S(2)}) collective-permute-start(s32[8]{0:T(128)S(1)} %copy-done.6), channel_id=1, source_target_pairs={{0,16},{16,0},{1,17},{17,1},{2,18},{18,2},{3,19},{19,3},{4,20},{20... | collective-permute-start | bytes 104 | tf_op jit(solution)/shard_map/ppermute | solution.py:548
  59.1 2.2 %copy-start.2 = (f32[16,5120]{1,0:T(8,128)S(1)}, f32[16,5120]{1,0:T(8,128)}, u32[]{:S(2)}) copy-start(f32[16,5120]{1,0:T(8,128)} %shift_ref.1) | copy-start | bytes 983044
  59.1 2.2 %copy-start.3 = (f32[16,5120]{1,0:T(8,128)S(1)}, f32[16,5120]{1,0:T(8,128)}, u32[]{:S(2)}) copy-start(f32[16,5120]{1,0:T(8,128)} %scale_ref.1) | copy-start | bytes 983044
  59.7 25.4 %collective-permute-start.1 = (bf16[8,264,128]{2,1,0:T(8,128)(2,1)S(1)}, bf16[8,264,128]{2,1,0:T(8,128)(2,1)S(1)}, u32[]{:S(2)}, u32[]{:S(2)}) collective-permute-start(bf16[8,264,128]{2,1,0:T(8,128)(2,1)S(1)} %choose.1), channel_id=1, source_target_pairs={{0,16},{16,0},{1,17},{17,1},{2,18},{18,2},{3,19},{19,3},{4,20},{20... | collective-permute-start | bytes 1622024 | tf_op jit(solution)/shard_map/ppermute | solution.py:594
  61.3 23.7 %copy-start.4 = (bf16[80,384]{1,0:T(8,128)(2,1)S(1)}, bf16[80,384]{1,0:T(8,128)(2,1)}, u32[]{:S(2)}) copy-start(bf16[80,384]{1,0:T(8,128)(2,1)} %get-tuple-element.10.gram_ref) | copy-start | bytes 184324
  61.3 23.7 %copy-start.5 = (f32[2,8,64]{2,1,0:T(8,128)S(1)}, f32[2,8,64]{2,1,0:T(8,128)}, u32[]{:S(2)}) copy-start(f32[2,8,64]{2,1,0:T(8,128)} %own_ref.1) | copy-start | bytes 12292

commit v6 on v5

--- a/solution.py
+++ b/solution.py
@@ -16,6 +16,7 @@
 TABLE_ROWS = 64
 BIAS_ROWS = 8
 LATENT_ROW = 4
+TOGETHER = 5
 VMEM_LIMIT = 20 << 20
 PREPARE_VMEM_LIMIT = 56 << 20
 
@@ -217,25 +218,29 @@
         return jnp.broadcast_to(value[None], (devices, 8, LANES)).reshape(size, LANES)
 
     total = jnp.zeros((size, LANES), jnp.float32)
-    for tile in range(tiles):
-        q, k, v, h = [
-            got_ref[
-                :,
-                table_rows + (kind * tiles + tile) * 8 : table_rows + (kind * tiles + tile) * 8 + 8,
-                :,
-            ].reshape(size, LANES)
-            for kind in range(4)
+    def states(kind, tile):
+        first = (kind * tiles + tile) * 8
+        return got_ref[:, table_rows + first : table_rows + first + 8, :].reshape(size, LANES)
+
+    for first in range(0, tiles, TOGETHER):
+        group = range(first, min(first + TOGETHER, tiles))
+        scores = [
+            jnp.where(allowed, nt_dot(states(0, t), states(1, t)) * score_scale, -jnp.inf)
+            for t in group
         ]
-        scores = jnp.where(allowed, nt_dot(q, k) * score_scale, -jnp.inf)
-        peak = jnp.max(scores, axis=-1, keepdims=True)
-        raised = jnp.exp(scores - peak)
-        weights = raised / jnp.sum(raised, axis=-1, keepdims=True)
-        attended = jnp.dot(
-            weights.astype(jnp.bfloat16), v, preferred_element_type=jnp.float32
-        ).astype(jnp.bfloat16)
-        residual = h.astype(jnp.float32) + modulation(0, tile) * attended.astype(jnp.float32)
-        residual_ref[tile] = residual
-        total = total + residual
+        peaks = [jnp.max(x, axis=-1, keepdims=True) for x in scores]
+        raised = [jnp.exp(x - peak) for x, peak in zip(scores, peaks)]
+        factors = [1.0 / jnp.sum(x, axis=-1, keepdims=True) for x in raised]
+        weights = [(x * factor).astype(jnp.bfloat16) for x, factor in zip(raised, factors)]
+        for tile, weight in zip(group, weights):
+            attended = jnp.dot(
+                weight, states(2, tile), preferred_element_type=jnp.float32
+            ).astype(jnp.bfloat16)
+            residual = states(3, tile).astype(jnp.float32) + modulation(
+                0, tile
+            ) * attended.astype(jnp.float32)
+            residual_ref[tile] = residual
+            total = total + residual
     mean = jnp.sum(group_sum(total), axis=-1, keepdims=True) * (1.0 / width)
     total = jnp.zeros((size, LANES), jnp.float32)
     for tile in range(tiles):

time: 87.2 us -> 86.1 us (0.987)
  Pallas kernels: 10.9 us -> 9.76 us
    pallas_call x1, Pallas kernels: 3.52 us -> 2.36 us  [one_stream_each(): pl.pallas_call(functools.partial(attend_kernel, table_rows=table_rows), o...]
  transfers between devices with their start and end apart: 3 -> 3, of which waited for: 2 -> 2; matrix products, arithmetic and copies ran while one was open for 0% -> 0% of each run, Pallas kernels for 4% -> 3%
where the time goes in v6:
time: 86.1 us; the launch traced here: 85.9 us
  waiting for transfers between devices  44.6 us (52%)
  blocking collectives  20.1 us (23%)
  starting transfers between devices  10.5 us (12%)
  Pallas kernels  9.76 us (11%)
    all_to_all x1, waiting for transfers between devices, one_stream_each(): got = lax.all_to_all(send, 'seq', split_axis=0, concat_axis=0, tiled=True)  42.6 us
    all_to_all x1, blocking collectives, one_stream_each(): lax.all_to_all(payload, 'seq', split_axis=0, concat_axis=0, tiled=True)  20.1 us
    all_to_all x1, starting transfers between devices, one_stream_each(): got = lax.all_to_all(send, 'seq', split_axis=0, concat_axis=0, tiled=True)  7.4 us
    pallas_call x1, Pallas kernels, one_stream_each(): pl.pallas_call(functools.partial(prepare_kernel, devices=devices, columns...  4.76 us
    pallas_call x1, Pallas kernels, one_stream_each(): pl.pallas_call(functools.partial(attend_kernel, table_rows=table_rows), o...  2.36 us
    ppermute x1, waiting for transfers between devices, one_stream_each(): other_ids = lax.ppermute(adapter_ids, 'rep', swap)  2.05 us
    pallas_call x1, Pallas kernels, one_stream_each(): pl.pallas_call(functools.partial(finish_kernel, devices=devices, columns=...  1.96 us
  transfers between devices with their start and end apart: 3, of which 2 were waited for; matrix products, arithmetic and copies ran while one was open for 0% of the time, Pallas kernels for 3%

profile of v6, /device:TPU:0, one launch (start us, length us, event | category | flops | bytes accessed | tf_op | source)
XLA Modules:
  0.0 85.9 jit_solution(11221510543180403316)
XLA Ops:
  0.6 4.8 %prepare.1 = (bf16[16,584,128]{2,1,0:T(8,128)(2,1)}, bf16[80,384]{1,0:T(8,128)(2,1)}) custom-call(bf16[2,16,5120]{2,1,0:T(8,128)(2,1)} %refs_0_.1, bf16[2,16,5120]{2,1,0:T(8,128)(2,1)} %refs_1_.1, bf16[2,16,5120]{2,1,0:T(8,128)(2,1)} %refs_2_.1, bf16[2,16,5120]{2,1,0:T(8,128)(2,1)} %refs_3_.1, bf16[64,5120]{1,0:T(8,128)(2,1)} %refs_4_.1, ...), custom_call_target="tpu_custom_call" | custom-call | tf_op jit(solution)/shard_map/prepare/pallas_call | solution.py:570
  5.4 0.0 copy-start.6
  5.4 7.4 %all-to-all-start = ((bf16[16,584,128]{2,1,0:T(8,128)(2,1)}), bf16[16,584,128]{2,1,0:T(8,128)(2,1)S(1)}, u32[]{:S(2)}, u32[]{:S(2)}) async-start(bf16[16,584,128]{2,1,0:T(8,128)(2,1)} %get-tuple-element.7), calls=%async_computation | async-start | bytes 4784128 | tf_op jit(solution)/shard_map/all_to_all | solution.py:589
  12.8 0.0 copy-done.6
  12.8 0.0 copy-start
  12.8 0.0 copy-start.1
  12.9 0.0 copy-start.7
  12.9 0.0 copy-start.8
  12.9 0.0 copy-start.9
  12.9 0.0 copy-start.10
  12.9 1.6 %collective-permute-start = (s32[8]{0:T(128)S(1)}, s32[8]{0:T(128)S(1)}, u32[]{:S(2)}, u32[]{:S(2)}) collective-permute-start(s32[8]{0:T(128)S(1)} %copy-done.6), channel_id=1, source_target_pairs={{0,16},{16,0},{1,17},{17,1},{2,18},{18,2},{3,19},{19,3},{4,20},{20... | collective-permute-start | bytes 104 | tf_op jit(solution)/shard_map/ppermute | solution.py:553
  14.5 2.0 %collective-permute-done.ids_ref = s32[8]{0:T(128)S(1)} collective-permute-done((s32[8]{0:T(128)S(1)}, s32[8]{0:T(128)S(1)}, u32[]{:S(2)}, u32[]{:S(2)}) %collective-permute-start) | collective-permute-done | bytes 64 | tf_op jit(solution)/shard_map/ppermute | solution.py:553
  16.5 42.6 %all-to-all-done.got_ref.near_ref = bf16[16,584,128]{2,1,0:T(8,128)(2,1)S(1)} async-done(((bf16[16,584,128]{2,1,0:T(8,128)(2,1)}), bf16[16,584,128]{2,1,0:T(8,128)(2,1)S(1)}, u32[]{:S(2)}, u32[]{:S(2)}) %all-to-all-start) | async-done | bytes 2392096 | tf_op jit(solution)/shard_map/all_to_all | solution.py:589
  59.1 0.0 copy-start.2
  59.1 0.0 copy-start.3
  59.1 0.6 choose.1
  59.7 1.6 %collective-permute-start.1 = (bf16[8,264,128]{2,1,0:T(8,128)(2,1)S(1)}, bf16[8,264,128]{2,1,0:T(8,128)(2,1)S(1)}, u32[]{:S(2)}, u32[]{:S(2)}) collective-permute-start(bf16[8,264,128]{2,1,0:T(8,128)(2,1)S(1)} %choose.1), channel_id=1, source_target_pairs={{0,16},{16,0},{1,17},{17,1},{2,18},{18,2},{3,19},{19,3},{4,20},{20... | collective-permute-start | bytes 1622024 | tf_op jit(solution)/shard_map/ppermute | solution.py:599
  61.2 0.0 copy-done
  61.2 0.0 copy-done.1
  61.2 0.0 copy-done.2
  61.2 0.0 copy-done.3
  61.2 0.1 modulate.1
  61.3 0.0 copy-start.4
  61.3 0.0 copy-start.5
  61.3 0.0 copy-done.7
  61.4 0.0 copy-done.8
  61.4 0.0 copy-done.9
  61.4 0.0 copy-done.10
  61.4 2.4 %attend.1 = f32[16,16,128]{2,1,0:T(8,128)S(1)} custom-call(s32[8]{0:T(128)S(1)} %copy-done.8, f32[8]{0:T(128)S(1)} %copy-done.9, s32[8]{0:T(128)S(1)} %copy-done.7, bf16[16,584,128]{2,1,0:T(8,128)(2,1)S(1)} %all-to-all-done.got_ref.near_ref, f32[3,8,1280]{2,1,0:T(8,128)S(1)} %get-tuple-element.8.rows_ref, bf16[256,1280]{1,0:T(8,128)(2,1)S(1)} %get-tuple-element.9.head_ref, ...), custom_call_target="tpu_custom_call" | custom-call | flops 1000000000 | bytes 4000000 | tf_op jit(solution)/shard_map/attend/pallas_call | solution.py:615
  63.8 20.1 %all_to_all.10 = f32[16,16,128]{2,1,0:T(8,128)S(1)} all-to-all(f32[16,16,128]{2,1,0:T(8,128)S(1)} %attend.1), channel_id=1, replica_groups=mesh['rep'=2,'seq'=16] {'seq'}, dimensions={0} | all-to-all | bytes 262144 | tf_op jit(solution)/shard_map/all_to_all | solution.py:638
  83.9 0.0 collective-permute-done.1.far_ref
  83.9 0.0 copy-done.4
  83.9 0.0 copy-done.5
  83.9 2.0 %finish.1 = (f32[2,8,64]{2,1,0:T(8,128)}, f32[2,8,64]{2,1,0:T(8,128)}, bf16[32,8,960]{2,1,0:T(8,128)(2,1)}) custom-call(s32[8]{0:T(128)S(1)} %copy-done.6, f32[256,128]{1,0:T(8,128)S(1)} %bitcast.11, s32[8]{0:T(128)S(1)} %copy-done.7, f32[2,8,64]{2,1,0:T(8,128)S(1)} %copy-done.5, bf16[80,384]{1,0:T(8,128)(2,1)S(1)} %copy-done.4, ...), custom_call_target="tpu_custom_call" | custom-call | tf_op jit(solution)/shard_map/finish/pallas_call | solution.py:641
Async XLA Ops:
  5.4 7.4 %copy-start.6 = (s32[8]{0:T(128)S(1)}, s32[8]{0:T(128)}, u32[]{:S(2)}) copy-start(s32[8]{0:T(128)} %ids_ref.1) | copy-start | bytes 100
  5.4 53.6 %all-to-all-start = ((bf16[16,584,128]{2,1,0:T(8,128)(2,1)}), bf16[16,584,128]{2,1,0:T(8,128)(2,1)S(1)}, u32[]{:S(2)}, u32[]{:S(2)}) async-start(bf16[16,584,128]{2,1,0:T(8,128)(2,1)} %get-tuple-element.7), calls=%async_computation | async-start | bytes 4784128 | tf_op jit(solution)/shard_map/all_to_all | solution.py:589
  12.8 48.4 %copy-start = (bf16[5120,64]{0,1:T(8,128)(2,1)S(1)}, bf16[5120,64]{0,1:T(8,128)(2,1)}, u32[]{:S(2)}) copy-start(bf16[5120,64]{0,1:T(8,128)(2,1)} %param.25) | copy-start | bytes 1966084
  12.8 48.4 %copy-start.1 = (f32[16,5120]{1,0:T(8,128)S(1)}, f32[16,5120]{1,0:T(8,128)}, u32[]{:S(2)}) copy-start(f32[16,5120]{1,0:T(8,128)} %gate_ref.1) | copy-start | bytes 983044
  12.9 48.5 %copy-start.7 = (s32[8]{0:T(128)S(1)}, s32[8]{0:T(128)}, u32[]{:S(2)}) copy-start(s32[8]{0:T(128)} %step_ref.3) | copy-start | bytes 100
  12.9 48.5 %copy-start.8 = (s32[8]{0:T(128)S(1)}, s32[8]{0:T(128)}, u32[]{:S(2)}) copy-start(s32[8]{0:T(128)} %lengths_ref.1) | copy-start | bytes 100
  12.9 48.5 %copy-start.9 = (f32[8]{0:T(128)S(1)}, f32[8]{0:T(128)}, u32[]{:S(2)}) copy-start(f32[8]{0:T(128)} %guidance_ref.1) | copy-start | bytes 100
  12.9 48.5 %copy-start.10 = (f32[64]{0:T(128)S(1)}, f32[64]{0:T(128)}, u32[]{:S(2)}) copy-start(f32[64]{0:T(128)} %param.26) | copy-start | bytes 772
  12.9 3.6 %collective-permute-start = (s32[8]{0:T(128)S(1)}, s32[8]{0:T(128)S(1)}, u32[]{:S(2)}, u32[]{:S(2)}) collective-permute-start(s32[8]{0:T(128)S(1)} %copy-done.6), channel_id=1, source_target_pairs={{0,16},{16,0},{1,17},{17,1},{2,18},{18,2},{3,19},{19,3},{4,20},{20... | collective-permute-start | bytes 104 | tf_op jit(solution)/shard_map/ppermute | solution.py:553
  59.1 2.2 %copy-start.2 = (f32[16,5120]{1,0:T(8,128)S(1)}, f32[16,5120]{1,0:T(8,128)}, u32[]{:S(2)}) copy-start(f32[16,5120]{1,0:T(8,128)} %shift_ref.1) | copy-start | bytes 983044
  59.1 2.2 %copy-start.3 = (f32[16,5120]{1,0:T(8,128)S(1)}, f32[16,5120]{1,0:T(8,128)}, u32[]{:S(2)}) copy-start(f32[16,5120]{1,0:T(8,128)} %scale_ref.1) | copy-start | bytes 983044
  59.7 24.2 %collective-permute-start.1 = (bf16[8,264,128]{2,1,0:T(8,128)(2,1)S(1)}, bf16[8,264,128]{2,1,0:T(8,128)(2,1)S(1)}, u32[]{:S(2)}, u32[]{:S(2)}) collective-permute-start(bf16[8,264,128]{2,1,0:T(8,128)(2,1)S(1)} %choose.1), channel_id=1, source_target_pairs={{0,16},{16,0},{1,17},{17,1},{2,18},{18,2},{3,19},{19,3},{4,20},{20... | collective-permute-start | bytes 1622024 | tf_op jit(solution)/shard_map/ppermute | solution.py:599
  61.3 22.6 %copy-start.4 = (bf16[80,384]{1,0:T(8,128)(2,1)S(1)}, bf16[80,384]{1,0:T(8,128)(2,1)}, u32[]{:S(2)}) copy-start(bf16[80,384]{1,0:T(8,128)(2,1)} %get-tuple-element.10.gram_ref) | copy-start | bytes 184324
  61.3 22.6 %copy-start.5 = (f32[2,8,64]{2,1,0:T(8,128)S(1)}, f32[2,8,64]{2,1,0:T(8,128)}, u32[]{:S(2)}) copy-start(f32[2,8,64]{2,1,0:T(8,128)} %own_ref.1) | copy-start | bytes 12292
